TPU v7x, 32 devices: a whole 2x2x4 slice. The times are simulated.
32 devices in a mesh: dp: 16 (over z, y, x), fsdp: 2 (over core).
Axes of the slice: x: 2, y: 2, z: 4, core: 2. Of those that a mesh axis runs over, the one named last changes fastest.
Arguments:
- tokens: bfloat16 [4096, 2048], P(('dp', 'fsdp')), may hold values from -6 to 6
- cotangent: bfloat16 [4096, 2048], P(('dp', 'fsdp')), may hold values from -6 to 6
- group_size: int32 [32], P(('dp', 'fsdp')), may hold values from 4 to 16, as said below
- prefix_len: int32 [32], P(('dp', 'fsdp')), may hold values from 16 to 32, as said below
- sol_len: int32 [32, 16], P(('dp', 'fsdp')), may hold values from 0 to 109, as said below
- ln1_gain: bfloat16 [2048], P(('dp', 'fsdp')), may hold values from 0.099609375 to 1.8984375
- ln1_bias: bfloat16 [2048], P(('dp', 'fsdp')), may hold values from -3 to 3
- w_qkv: bfloat16 [2048, 6144], P(('dp', 'fsdp')), may hold values from -0.125 to 0.125
- q_bias: bfloat16 [2048], P(('dp', 'fsdp')), may hold values from -3 to 3
- v_bias: bfloat16 [2048], P(('dp', 'fsdp')), may hold values from -3 to 3
- w_out: bfloat16 [2048, 2048], P(('dp', 'fsdp')), may hold values from -1 to 1
- out_bias: bfloat16 [2048], P(('dp', 'fsdp')), may hold values from -3 to 3
- ln2_gain: bfloat16 [2048], P(('dp', 'fsdp')), may hold values from 0.099609375 to 1.8984375
- ln2_bias: bfloat16 [2048], P(('dp', 'fsdp')), may hold values from -3 to 3
- w_up: bfloat16 [2048, 8192], P(('dp', 'fsdp')), may hold values from -0.125 to 0.125
- up_bias: bfloat16 [8192], P(('dp', 'fsdp')), may hold values from -3 to 3
- w_down: bfloat16 [8192, 2048], P(('dp', 'fsdp')), may hold values from -0.0625 to 0.0625
- down_bias: bfloat16 [2048], P(('dp', 'fsdp')), may hold values from -3 to 3
Outputs:
- layer_out: bfloat16 [4096, 2048], P(('dp', 'fsdp'))
- tokens_grad: bfloat16 [4096, 2048], P(('dp', 'fsdp'))
- ln1_gain_grad: float32 [2048], P(('dp', 'fsdp'))
- ln1_bias_grad: float32 [2048], P(('dp', 'fsdp'))
- w_qkv_grad: float32 [2048, 6144], P(('dp', 'fsdp'))
- q_bias_grad: float32 [2048], P(('dp', 'fsdp'))
- v_bias_grad: float32 [2048], P(('dp', 'fsdp'))
- w_out_grad: float32 [2048, 2048], P(('dp', 'fsdp'))
- out_bias_grad: float32 [2048], P(('dp', 'fsdp'))
- ln2_gain_grad: float32 [2048], P(('dp', 'fsdp'))
- ln2_bias_grad: float32 [2048], P(('dp', 'fsdp'))
- w_up_grad: float32 [2048, 8192], P(('dp', 'fsdp'))
- up_bias_grad: float32 [8192], P(('dp', 'fsdp'))
- w_down_grad: float32 [8192, 2048], P(('dp', 'fsdp'))
- down_bias_grad: float32 [2048], P(('dp', 'fsdp'))
Inputs may be any that keep to these rules, and one draw needn't show every extreme that they name: `group_size`: some group has 16 solutions and some group 4. `prefix_len`: some group has a prefix of 128 // 8 tokens and some one of 128 // 4. `sol_len`: entries from group_size[g] on are 0, the others 1 or more; a group's prefix and solutions together take at most 128 slots, exactly 128 in some group, and half of them or more in every group; some solution reaches the most.
All inputs are finite; a program needn't handle non-finite values.
Results may differ from a plain program's by a relative error of at most 0.012.
Values may be sent and summed in bfloat16 or wider, within the bound.
A program may use at most 384 MiB of HBM per device.

v0:
```python
import jax
import jax.numpy as jnp
from jax import lax
from jax.sharding import PartitionSpec as P

HEADS = 16


EPSILON = 1e-05


def normalize(values_in, gain, shift):
    center = values_in - jnp.mean(values_in, axis=-1, keepdims=True)
    spread = jnp.mean(center * center, axis=-1, keepdims=True)
    return center * lax.rsqrt(spread + EPSILON) * gain + shift


def segment_of(group_count, prefix, lengths, slots):
    slot_index = jnp.arange(lengths.shape[-1], dtype=jnp.int32)
    used = lengths * (slot_index < group_count).astype(jnp.int32)
    bounds = prefix + jnp.cumsum(used)
    total = prefix + jnp.sum(used)
    places = jnp.arange(slots, dtype=jnp.int32)
    inside = 1 + jnp.sum((bounds[None, :] <= places[:, None]).astype(jnp.int32), axis=1)
    return jnp.where(places < prefix, 0, jnp.where(places < total, inside, -1))


def allowed_pairs(segment):
    places = jnp.arange(segment.shape[0], dtype=jnp.int32)
    later = places[None, :] <= places[:, None]
    same = (segment[None, :] == 0) | (segment[None, :] == segment[:, None])
    alive = segment[:, None] >= 0
    allowed = later & same & alive | (places[None, :] == places[:, None])
    return (allowed, (segment >= 0).astype(jnp.float32))


def gelu_tanh(inner_value):
    return jax.nn.gelu(inner_value, approximate=True)


def local(
    tokens,
    cotangent,
    group_size,
    prefix_len,
    sol_len,
    ln1_gain,
    ln1_bias,
    w_qkv,
    q_bias,
    v_bias,
    w_out,
    out_bias,
    ln2_gain,
    ln2_bias,
    w_up,
    up_bias,
    w_down,
    down_bias,
):
    slots, width = tokens.shape
    shard_rows = w_up.shape[0]
    hidden = w_up.shape[1]
    unit_ratio = hidden // width
    head_size = width // HEADS
    score_scale = head_size ** (-0.5)
    segment = segment_of(group_size[0], prefix_len[0], sol_len[0], slots)
    allowed, live_rows = allowed_pairs(segment)
    inputs = tokens.astype(jnp.float32)
    attn_whole = (
        lax.all_gather(w_qkv, ("dp", "fsdp"), axis=0, tiled=True),
        lax.all_gather(w_out, ("dp", "fsdp"), axis=0, tiled=True),
        lax.all_gather(ln1_gain, ("dp", "fsdp"), axis=0, tiled=True),
        lax.all_gather(ln1_bias, ("dp", "fsdp"), axis=0, tiled=True),
        lax.all_gather(q_bias, ("dp", "fsdp"), axis=0, tiled=True),
        lax.all_gather(v_bias, ("dp", "fsdp"), axis=0, tiled=True),
        lax.all_gather(out_bias, ("dp", "fsdp"), axis=0, tiled=True),
    )
    qkv_rows, out_rows, gain_first, shift_first, query_bias, value_bias, out_shift = attn_whole
    normed_first = normalize(
        inputs, gain_first.astype(jnp.float32), shift_first.astype(jnp.float32)
    ).astype(jnp.bfloat16)
    projected = jnp.dot(normed_first, qkv_rows, preferred_element_type=jnp.float32)
    query = (projected[:, :width] + query_bias.astype(jnp.float32)).astype(jnp.bfloat16)
    keys = projected[:, width : 2 * width].astype(jnp.bfloat16)
    values = (projected[:, 2 * width :] + value_bias.astype(jnp.float32)).astype(jnp.bfloat16)
    query_heads = query.reshape(slots, HEADS, head_size)
    key_heads = keys.reshape(slots, HEADS, head_size)
    value_heads = values.reshape(slots, HEADS, head_size)
    scores = (
        jnp.einsum("qhd,khd->hqk", query_heads, key_heads, preferred_element_type=jnp.float32)
        * score_scale
    )
    scores = jnp.where(allowed[None], scores, jnp.float32(-1e30))
    peak = jnp.max(scores, axis=-1, keepdims=True)
    exponent = jnp.exp(scores - peak)
    attn_probs = exponent / jnp.sum(exponent, axis=-1, keepdims=True)
    probs_low = attn_probs.astype(jnp.bfloat16)
    context_full = jnp.einsum(
        "hqk,khd->qhd", probs_low, value_heads, preferred_element_type=jnp.float32
    )
    context = (context_full.reshape(slots, width) * live_rows[:, None]).astype(jnp.bfloat16)
    residual = (
        inputs
        + jnp.dot(context, out_rows, preferred_element_type=jnp.float32)
        + out_shift.astype(jnp.float32)
    )
    mlp_whole = (
        lax.all_gather(w_up, ("dp", "fsdp"), axis=0, tiled=True),
        lax.all_gather(
            w_down.reshape(shard_rows, unit_ratio * width), ("dp", "fsdp"), axis=0, tiled=True
        ),
        lax.all_gather(ln2_gain, ("dp", "fsdp"), axis=0, tiled=True),
        lax.all_gather(ln2_bias, ("dp", "fsdp"), axis=0, tiled=True),
        lax.all_gather(up_bias.reshape(shard_rows, unit_ratio), ("dp", "fsdp"), axis=0, tiled=True),
        lax.all_gather(down_bias, ("dp", "fsdp"), axis=0, tiled=True),
    )
    up_rows, down_folded, gain_second, shift_second, up_folded, down_shift = mlp_whole
    down_rows = down_folded.reshape(hidden, width)
    normed_second = normalize(
        residual, gain_second.astype(jnp.float32), shift_second.astype(jnp.float32)
    ).astype(jnp.bfloat16)
    up_proj = jnp.dot(
        normed_second, up_rows, preferred_element_type=jnp.float32
    ) + up_folded.reshape(hidden).astype(jnp.float32)
    activated = gelu_tanh(up_proj).astype(jnp.bfloat16)
    mlp_branch = jnp.dot(
        activated, down_rows, preferred_element_type=jnp.float32
    ) + down_shift.astype(jnp.float32)
    layer_out = (residual + mlp_branch).astype(jnp.bfloat16)
    up_back, down_back_folded, gain_second_back = (
        lax.all_gather(w_up, ("dp", "fsdp"), axis=0, tiled=True),
        lax.all_gather(
            w_down.reshape(shard_rows, unit_ratio * width), ("dp", "fsdp"), axis=0, tiled=True
        ),
        lax.all_gather(ln2_gain, ("dp", "fsdp"), axis=0, tiled=True),
    )
    down_back = down_back_folded.reshape(hidden, width)
    down_bias_term = jnp.sum(cotangent, axis=0, dtype=jnp.float32)
    down_term = jnp.einsum("ti,td->id", activated, cotangent, preferred_element_type=jnp.float32)
    d_activated = jnp.einsum("td,id->ti", cotangent, down_back, preferred_element_type=jnp.float32)
    _, gelu_pull = jax.vjp(gelu_tanh, up_proj)
    d_up = gelu_pull(d_activated)[0].astype(jnp.bfloat16)
    up_bias_term = jnp.sum(d_up, axis=0, dtype=jnp.float32)
    up_term = jnp.einsum("tc,ti->ci", normed_second, d_up, preferred_element_type=jnp.float32)
    d_normed = jnp.einsum("ti,ci->tc", d_up, up_back, preferred_element_type=jnp.float32)
    zero_shift = jnp.zeros((width,), jnp.float32)
    _, second_pull = jax.vjp(normalize, residual, gain_second_back.astype(jnp.float32), zero_shift)
    d_residual_norm, gain_second_term, shift_second_term = second_pull(d_normed)
    d_residual = cotangent.astype(jnp.float32) + d_residual_norm
    mlp_sums = (
        lax.psum_scatter(up_term, ("dp", "fsdp"), scatter_dimension=0, tiled=True),
        lax.psum_scatter(
            down_term.reshape(width, unit_ratio * width),
            ("dp", "fsdp"),
            scatter_dimension=0,
            tiled=True,
        ),
        lax.psum_scatter(gain_second_term, ("dp", "fsdp"), scatter_dimension=0, tiled=True),
        lax.psum_scatter(shift_second_term, ("dp", "fsdp"), scatter_dimension=0, tiled=True),
        lax.psum_scatter(
            up_bias_term.reshape(width, unit_ratio), ("dp", "fsdp"), scatter_dimension=0, tiled=True
        ),
        lax.psum_scatter(down_bias_term, ("dp", "fsdp"), scatter_dimension=0, tiled=True),
    )
    w_up_grad, down_grad_folded, ln2_gain_grad, ln2_bias_grad, up_grad_folded, down_bias_grad = (
        mlp_sums
    )
    qkv_back, out_back, gain_first_back = (
        lax.all_gather(w_qkv, ("dp", "fsdp"), axis=0, tiled=True),
        lax.all_gather(w_out, ("dp", "fsdp"), axis=0, tiled=True),
        lax.all_gather(ln1_gain, ("dp", "fsdp"), axis=0, tiled=True),
    )
    d_branch = d_residual.astype(jnp.bfloat16)
    out_bias_term = jnp.sum(d_branch, axis=0, dtype=jnp.float32)
    out_term = jnp.einsum("tc,td->cd", context, d_branch, preferred_element_type=jnp.float32)
    d_context_full = jnp.einsum("td,cd->tc", d_branch, out_back, preferred_element_type=jnp.float32)
    d_context = (
        (d_context_full * live_rows[:, None]).astype(jnp.bfloat16).reshape(slots, HEADS, head_size)
    )
    d_probs = jnp.einsum("qhd,khd->hqk", d_context, value_heads, preferred_element_type=jnp.float32)
    d_values_full = jnp.einsum(
        "hqk,qhd->khd", probs_low, d_context, preferred_element_type=jnp.float32
    )
    row_inner = jnp.sum(attn_probs * d_probs, axis=-1, keepdims=True)
    d_scores = (attn_probs * (d_probs - row_inner)).astype(jnp.bfloat16)
    d_query = (
        (
            jnp.einsum("hqk,khd->qhd", d_scores, key_heads, preferred_element_type=jnp.float32)
            * score_scale
        )
        .reshape(slots, width)
        .astype(jnp.bfloat16)
    )
    d_keys = (
        (
            jnp.einsum("hqk,qhd->khd", d_scores, query_heads, preferred_element_type=jnp.float32)
            * score_scale
        )
        .reshape(slots, width)
        .astype(jnp.bfloat16)
    )
    d_values = d_values_full.reshape(slots, width).astype(jnp.bfloat16)
    query_bias_term = jnp.sum(d_query, axis=0, dtype=jnp.float32)
    value_bias_term = jnp.sum(d_values, axis=0, dtype=jnp.float32)
    d_qkv = jnp.concatenate([d_query, d_keys, d_values], axis=1)
    qkv_term = jnp.einsum("tc,tj->cj", normed_first, d_qkv, preferred_element_type=jnp.float32)
    d_first = jnp.einsum("tj,cj->tc", d_qkv, qkv_back, preferred_element_type=jnp.float32)
    _, first_pull = jax.vjp(normalize, inputs, gain_first_back.astype(jnp.float32), zero_shift)
    d_norm_input, gain_first_term, shift_first_term = first_pull(d_first)
    tokens_grad = (d_residual + d_norm_input).astype(jnp.bfloat16)
    attn_sums = (
        lax.psum_scatter(qkv_term, ("dp", "fsdp"), scatter_dimension=0, tiled=True),
        lax.psum_scatter(out_term, ("dp", "fsdp"), scatter_dimension=0, tiled=True),
        lax.psum_scatter(gain_first_term, ("dp", "fsdp"), scatter_dimension=0, tiled=True),
        lax.psum_scatter(shift_first_term, ("dp", "fsdp"), scatter_dimension=0, tiled=True),
        lax.psum_scatter(query_bias_term, ("dp", "fsdp"), scatter_dimension=0, tiled=True),
        lax.psum_scatter(value_bias_term, ("dp", "fsdp"), scatter_dimension=0, tiled=True),
        lax.psum_scatter(out_bias_term, ("dp", "fsdp"), scatter_dimension=0, tiled=True),
    )
    (
        w_qkv_grad,
        w_out_grad,
        ln1_gain_grad,
        ln1_bias_grad,
        q_bias_grad,
        v_bias_grad,
        out_bias_grad,
    ) = attn_sums
    w_down_grad = down_grad_folded.reshape(shard_rows * unit_ratio, width)
    up_bias_grad = up_grad_folded.reshape(shard_rows * unit_ratio)
    return (
        layer_out,
        tokens_grad,
        ln1_gain_grad,
        ln1_bias_grad,
        w_qkv_grad,
        q_bias_grad,
        v_bias_grad,
        w_out_grad,
        out_bias_grad,
        ln2_gain_grad,
        ln2_bias_grad,
        w_up_grad,
        up_bias_grad,
        w_down_grad,
        down_bias_grad,
    )


def solution(mesh):
    return jax.shard_map(
        local,
        mesh=mesh,
        in_specs=(
            P(("dp", "fsdp"), None),
            P(("dp", "fsdp"), None),
            P(("dp", "fsdp")),
            P(("dp", "fsdp")),
            P(("dp", "fsdp"), None),
            P(("dp", "fsdp")),
            P(("dp", "fsdp")),
            P(("dp", "fsdp"), None),
            P(("dp", "fsdp")),
            P(("dp", "fsdp")),
            P(("dp", "fsdp"), None),
            P(("dp", "fsdp")),
            P(("dp", "fsdp")),
            P(("dp", "fsdp")),
            P(("dp", "fsdp"), None),
            P(("dp", "fsdp")),
            P(("dp", "fsdp"), None),
            P(("dp", "fsdp")),
        ),
        out_specs=(
            P(("dp", "fsdp"), None),
            P(("dp", "fsdp"), None),
            P(("dp", "fsdp")),
            P(("dp", "fsdp")),
            P(("dp", "fsdp"), None),
            P(("dp", "fsdp")),
            P(("dp", "fsdp")),
            P(("dp", "fsdp"), None),
            P(("dp", "fsdp")),
            P(("dp", "fsdp")),
            P(("dp", "fsdp")),
            P(("dp", "fsdp"), None),
            P(("dp", "fsdp")),
            P(("dp", "fsdp"), None),
            P(("dp", "fsdp")),
        ),
        check_vma=False,
    )
```

profile of v0, /device:TPU:0, one launch (start us, length us, event | category | flops | bytes accessed | tf_op | source)
XLA Modules:
  0.0 3028.5 jit_solution(16984849353963941246)
XLA Ops:
  14.2 44.6 %all-reduce.17 = (bf16[2048]{0:T(1024)(128)(2,1)S(1)}, bf16[2048]{0:T(1024)(128)(2,1)S(1)}, bf16[2048]{0:T(1024)(128)(2,1)S(1)}, bf16[2048]{0:T(1024)(128)(2,1)S...) all-reduce(bf16[2048]{0:T(1024)(128)(2,1)S(1)} %dynamic-update-slic, ...), channel_id=1, replica_groups=mesh['dp'=16,'fsdp'=2] {'dp','fsdp'}, use_global_device_ids=true, to_apply=%add.4 | all-reduce | flops 16384 | bytes 65536
  60.4 40.4 %all-gather = bf16[32,64,4]{1,2,0:T(4,128)(2,1)S(1)} all-gather(bf16[1,64,4]{1,2,0:T(4,128)(2,1)S(1)} %copy.113), channel_id=1, replica_groups=mesh['dp'=16,'fsdp'=2] {'dp','fsdp'}, dimensions={0}, use_global_device_ids=true | all-gather | bytes 16896 | tf_op jit(solution)/shard_map/all_gather | solution.py:115
  104.1 65.4 %all-gather.6.cloned.1.call-done = bf16[2048,6144]{1,0:T(8,128)(2,1)} async-done(((bf16[64,6144]{1,0:T(8,128)(2,1)}), bf16[2048,6144]{1,0:T(8,128)(2,1)}) %all-gather.6.cloned.1.call-update) | async-done | bytes 25165840 | tf_op jit(solution)/shard_map/all_gather | solution.py:71
  169.4 10.6 fusion.55
  185.7 61.9 %all-gather.8.cloned.1.call-done = bf16[2048,2048]{1,0:T(8,128)(2,1)} async-done(((bf16[64,2048]{1,0:T(8,128)(2,1)}), bf16[2048,2048]{1,0:T(8,128)(2,1)}) %all-gather.8.cloned.1.call-update) | async-done | bytes 8388624 | tf_op jit(solution)/shard_map/all_gather | solution.py:72
  252.7 191.1 %all-gather.12.cloned.1.call-done = bf16[2048,8192]{1,0:T(8,128)(2,1)} async-done(((bf16[64,8192]{1,0:T(8,128)(2,1)}), bf16[2048,8192]{1,0:T(8,128)(2,1)}) %all-gather.12.cloned.1.call-update) | async-done | bytes 33554448 | tf_op jit(solution)/shard_map/all_gather | solution.py:110
  443.8 55.4 %reshape.319 = bf16[8192,2048]{1,0:T(8,128)(2,1)} reshape(bf16[2048,8192]{1,0:T(8,128)(2,1)} %all-gather.12.cloned.1.call-done) | data formatting | bytes 67108864 | tf_op jit(solution)/shard_map/reshape | solution.py:119
  499.2 17.4 fusion.66
  516.6 122.3 %all-gather.10.cloned.1.call-done = bf16[2048,8192]{1,0:T(8,128)(2,1)} async-done(((bf16[64,8192]{1,0:T(8,128)(2,1)}), bf16[2048,8192]{1,0:T(8,128)(2,1)}) %all-gather.10.cloned.1.call-update) | async-done | bytes 33554448 | tf_op jit(solution)/shard_map/all_gather | solution.py:109
  638.9 18.2 convert_reduce_fusion
  657.0 19.8 multiply_reduce_fusion
  680.2 7.1 fusion.10
  702.5 15.1 fusion.60
  725.3 25.6 fusion.59
  750.9 79.4 %reshape.323 = f32[2048,8192]{1,0:T(8,128)} reshape(f32[8192,2048]{1,0:T(8,128)} %fusion.59) | data formatting | bytes 134217728 | tf_op jit(solution)/shard_map/reshape | solution.py:154
  831.7 8.2 fusion.53
  841.3 20.8 fusion.32
  862.8 25.1 fusion.58
  888.6 17.7 fusion.11
  916.4 67.9 %reduce-scatter.12.cloned.1.call-done = f32[64,4]{1,0:T(8,128)} async-done(((f32[2048,4]{1,0:T(8,128)}), f32[64,4]{1,0:T(8,128)}) %reduce-scatter.12.cloned.1.call-update) | async-done | bytes 1040 | tf_op jit(solution)/shard_map/reduce_scatter | solution.py:161
  985.8 699.5 %reduce-scatter.14.cloned.1.call-done = f32[64,8192]{1,0:T(8,128)} async-done(((f32[2048,8192]{1,0:T(8,128)}), f32[64,8192]{1,0:T(8,128)}) %reduce-scatter.14.cloned.1.call-update) | async-done | bytes 2097168 | tf_op jit(solution)/shard_map/reduce_scatter | solution.py:153
  1688.1 190.7 %reduce-scatter.8.cloned.1.call-done = f32[64,2048]{1,0:T(8,128)} async-done(((f32[2048,2048]{1,0:T(8,128)}), f32[64,2048]{1,0:T(8,128)}) %reduce-scatter.8.cloned.1.call-update) | async-done | bytes 524304 | tf_op jit(solution)/shard_map/reduce_scatter | solution.py:214
  1878.8 437.9 %reduce-scatter.6.cloned.1.call-done = f32[64,6144]{1,0:T(8,128)} async-done(((f32[2048,6144]{1,0:T(8,128)}), f32[64,6144]{1,0:T(8,128)}) %reduce-scatter.6.cloned.1.call-update) | async-done | bytes 1572880 | tf_op jit(solution)/shard_map/reduce_scatter | solution.py:213
  2316.7 704.5 %reduce-scatter.10.cloned.1.call-done = f32[64,8192]{1,0:T(8,128)} async-done(((f32[2048,8192]{1,0:T(8,128)}), f32[64,8192]{1,0:T(8,128)}) %reduce-scatter.10.cloned.1.call-update) | async-done | bytes 2097168 | tf_op jit(solution)/shard_map/reduce_scatter | solution.py:152
  (165 shorter events, 64.8 us)
Async XLA Ops:
  7.2 5.2 copy-start.23
  7.2 5.5 copy-start.24
  7.2 5.7 copy-start.25
  7.2 6.0 copy-start.26
  7.2 6.2 copy-start.27
  7.2 6.4 copy-start.28
  7.3 6.7 copy-start.29
  7.3 52.2 %copy-start.30 = (s32[1,16]{1,0:T(1,128)S(1)}, s32[1,16]{1,0:T(1,128)}, u32[]{:S(2)}) copy-start(s32[1,16]{1,0:T(1,128)} %param.22) | copy-start | bytes 196
  7.3 53.0 %copy-start.21 = (bf16[256]{0:T(256)(128)(2,1)S(1)}, bf16[256]{0:T(256)(128)(2,1)}, u32[]{:S(2)}) copy-start(bf16[256]{0:T(256)(128)(2,1)} %param.33) | copy-start | bytes 1540
  7.3 96.2 %copy-start = (bf16[128,2048]{1,0:T(8,128)(2,1)S(1)}, bf16[128,2048]{1,0:T(8,128)(2,1)}, u32[]{:S(2)}) copy-start(bf16[128,2048]{1,0:T(8,128)(2,1)} %param.18) | copy-start | bytes 1572868
  7.3 162.1 %all-gather.6.cloned.1.call-start = ((), (), s32[]{:S(2)}) async-start(), calls=%async_computation.5 | async-start | bytes 25952256 | tf_op jit(solution)/shard_map/all_gather | solution.py:71
  8.0 239.5 %all-gather.8.cloned.1.call-start = ((), (), s32[]{:S(2)}) async-start(), calls=%async_computation.6 | async-start | bytes 8650752 | tf_op jit(solution)/shard_map/all_gather | solution.py:72
  8.8 435.0 %all-gather.12.cloned.1.call-start = ((), (), s32[]{:S(2)}) async-start(), calls=%async_computation.8 | async-start | bytes 34603008 | tf_op jit(solution)/shard_map/all_gather | solution.py:110
  11.5 627.4 %all-gather.10.cloned.1.call-start = ((), (), s32[]{:S(2)}) async-start(), calls=%async_computation.7 | async-start | bytes 34603008 | tf_op jit(solution)/shard_map/all_gather | solution.py:109
  12.1 894.2 %all-reduce.20.cloned.1.call-start = ((), (), s32[]{:S(2)}) async-start(), calls=%async_computation.14 | async-start | bytes 131072
  58.8 110.6 %copy-start.16 = (f32[2048]{0:T(1024)}, f32[2048]{0:T(1024)S(1)}, u32[]{:S(2)}) copy-start(f32[2048]{0:T(1024)S(1)} %convert_element_type.143) | copy-start | bytes 24580
  101.9 537.0 %copy-start.18 = (f32[2048]{0:T(1024)}, f32[2048]{0:T(1024)S(1)}, u32[]{:S(2)}) copy-start(f32[2048]{0:T(1024)S(1)} %convert_element_type.155) | copy-start | bytes 24580
  185.7 66.7 %copy-start.1 = (f32[128,2048]{1,0:T(8,128)}, f32[128,2048]{1,0:T(8,128)S(1)}, u32[]{:S(2)}) copy-start(f32[128,2048]{1,0:T(8,128)S(1)} %copy.112) | copy-start | bytes 3145732
  252.7 246.5 %copy-start.3 = (bf16[128,2048]{1,0:T(8,128)(2,1)S(1)}, bf16[128,2048]{1,0:T(8,128)(2,1)}, u32[]{:S(2)}) copy-start(bf16[128,2048]{1,0:T(8,128)(2,1)} %param.19) | copy-start | bytes 1572868
  723.2 261.2 %reduce-scatter.12.cloned.1.call-start = ((), (), s32[]{:S(2)}) async-start(), calls=%async_computation.12 | async-start | bytes 1081344 | tf_op jit(solution)/shard_map/reduce_scatter | solution.py:161
  725.3 960.0 %reduce-scatter.14.cloned.1.call-start = ((), (), s32[]{:S(2)}) async-start(), calls=%async_computation.13 | async-start | bytes 69206016 | tf_op jit(solution)/shard_map/reduce_scatter | solution.py:153
  830.3 1048.5 %reduce-scatter.8.cloned.1.call-start = ((), (), s32[]{:S(2)}) async-start(), calls=%async_computation.10 | async-start | bytes 17301504 | tf_op jit(solution)/shard_map/reduce_scatter | solution.py:214
  839.9 1476.8 %reduce-scatter.6.cloned.1.call-start = ((), (), s32[]{:S(2)}) async-start(), calls=%async_computation.9 | async-start | bytes 51904512 | tf_op jit(solution)/shard_map/reduce_scatter | solution.py:213
  862.1 2159.2 %reduce-scatter.10.cloned.1.call-start = ((), (), s32[]{:S(2)}) async-start(), calls=%async_computation.11 | async-start | bytes 69206016 | tf_op jit(solution)/shard_map/reduce_scatter | solution.py:152
  (17 other events, 35.7 us)
Sparse Core Ops, SparseCore 0:
  11.0 158.4 all-gather.5
  172.3 75.2 all-gather.7
  251.0 192.7 all-gather.11
  446.5 192.3 all-gather.9
  723.3 120.6 all-reduce.19
  846.7 137.6 reduce-scatter.11
  986.7 698.5 reduce-scatter.13
  1688.1 190.6 reduce-scatter.7
  1885.8 430.8 reduce-scatter.5
  2319.5 701.7 reduce-scatter.9
where the time goes:
time: 3040 us; the launch traced here: 3030 us
  waiting for transfers between devices  2540 us (84%)
  matrix products  201 us (7%)
  local copies, waits for them, and re-layouts  170 us (6%)
  blocking collectives  85 us (3%)
    reduce_scatter x1, waiting for transfers between devices, local(): lax.psum_scatter(up_term, ('dp', 'fsdp'), scatter_dimension=0, tiled=True)  705 us
    reduce_scatter x1, waiting for transfers between devices, local(): lax.psum_scatter(down_term.reshape(width, unit_ratio * width), ('dp', 'fs...  699 us
    reduce_scatter x1, waiting for transfers between devices, local(): lax.psum_scatter(qkv_term, ('dp', 'fsdp'), scatter_dimension=0, tiled=True)  438 us
    all_gather x1, waiting for transfers between devices, local(): lax.all_gather(w_down.reshape(shard_rows, unit_ratio * width), ('dp', 'fs...  191 us
    reduce_scatter x1, waiting for transfers between devices, local(): lax.psum_scatter(out_term, ('dp', 'fsdp'), scatter_dimension=0, tiled=True)  191 us
    all_gather x1, waiting for transfers between devices, local(): lax.all_gather(w_up, ('dp', 'fsdp'), axis=0, tiled=True)  122 us
    reshape x1, local copies, waits for them, and re-layouts, local(): down_term.reshape(width, unit_ratio * width)  79.4 us
    reduce_scatter x1, waiting for transfers between devices, local(): lax.psum_scatter(up_bias_term.reshape(width, unit_ratio), ('dp', 'fsdp'),...  67.9 us
  transfers between devices with their start and end apart: 10, of which 9 were waited for; matrix products, arithmetic and copies ran while one was open for 10% of the time, Pallas kernels for 0%

commit v1 on v0

v1 whole, which is shorter than its diff:
```python
import functools

import jax
import jax.numpy as jnp
from jax import lax
from jax.sharding import Mesh
from jax.sharding import PartitionSpec as P

HEADS = 16
EPSILON = 1e-05
BF = jnp.bfloat16
F32 = jnp.float32
T_AXES = ("p", "x")
R_AXES = ("h", "y", "w", "c")
ALL = ("h", "p", "y", "x", "w", "c")


def ln_parts(values_in):
    center = values_in - jnp.mean(values_in, axis=-1, keepdims=True)
    spread = jnp.mean(center * center, axis=-1, keepdims=True)
    scale = lax.rsqrt(spread + EPSILON)
    return center * scale, scale


def ln_back(d_out, gain, unit, scale):
    d_unit = d_out * gain
    mean_d = jnp.mean(d_unit, axis=-1, keepdims=True)
    mean_du = jnp.mean(d_unit * unit, axis=-1, keepdims=True)
    return (d_unit - mean_d - unit * mean_du) * scale


def segment_of(group_count, prefix, lengths, slots):
    slot_index = jnp.arange(lengths.shape[-1], dtype=jnp.int32)
    used = lengths * (slot_index < group_count).astype(jnp.int32)
    total = prefix + jnp.sum(used)
    before = (slot_index[None, :] <= slot_index[:, None]).astype(jnp.int32)
    bounds = prefix + jnp.sum(used[None, :] * before, axis=1)
    places = jnp.arange(slots, dtype=jnp.int32)
    inside = 1 + jnp.sum((bounds[None, :] <= places[:, None]).astype(jnp.int32), axis=1)
    return jnp.where(places < prefix, 0, jnp.where(places < total, inside, -1))


def gelu_tanh(inner_value):
    return jax.nn.gelu(inner_value, approximate=True)


def dot(a, b, dims):
    return lax.dot_general(a, b, (dims, ((), ())), preferred_element_type=F32)


def swap(x, axes, mask, sizes):
    count = 1
    for name in axes:
        count *= sizes[name]
    return lax.ppermute(x, axes, [(i, i ^ mask) for i in range(count)])


def gather_t(x, sizes):
    return jnp.stack([x] + [swap(x, T_AXES, m, sizes) for m in (1, 2, 3)])


def scatter_t(parts, sizes):
    total = parts[0]
    for m in (1, 2, 3):
        total = total + swap(parts[m].astype(BF), T_AXES, m, sizes).astype(F32)
    return total


def reduce_axis(x, axis, name, sizes):
    count = sizes[name]
    me = lax.axis_index(name)
    total = lax.dynamic_index_in_dim(x, me, axis, keepdims=False).astype(F32)
    for m in range(1, count):
        piece = lax.dynamic_index_in_dim(x, me ^ m, axis, keepdims=False).astype(BF)
        total = total + swap(piece, (name,), m, sizes).astype(F32)
    return total


def local(
    sizes,
    tokens,
    cotangent,
    group_size,
    prefix_len,
    sol_len,
    ln1_gain,
    ln1_bias,
    w_qkv,
    q_bias,
    v_bias,
    w_out,
    out_bias,
    ln2_gain,
    ln2_bias,
    w_up,
    up_bias,
    w_down,
    down_bias,
):
    nh, np_, ny, nx, nw, nc = (sizes[a] for a in ALL)
    nt = np_ * nx
    slots, width = tokens.shape
    rows = w_qkv.shape[0]
    hidden = w_up.shape[1]
    ff_rows = w_down.shape[0]
    ff_t = hidden // nt
    head = width // HEADS
    heads_t = HEADS // nt
    cols_t = width // nt
    score_scale = head ** (-0.5)
    pi, xi = lax.axis_index("p"), lax.axis_index("x")

    def mine(v, axes):
        for axis, at in zip(axes, (pi, xi)):
            v = lax.dynamic_index_in_dim(v, at, axis, keepdims=True)
        return v

    segment = segment_of(group_size[0], prefix_len[0], sol_len[0], slots)
    unit = hidden // width
    vectors = (ln1_gain, ln1_bias, q_bias, v_bias, out_bias, ln2_gain, ln2_bias, down_bias, up_bias)
    small = jnp.concatenate(vectors + (segment.astype(BF),))
    small_all = lax.all_gather(small, ALL, axis=0)
    at = 0
    full = []
    for v in vectors:
        full.append(small_all[:, at : at + v.shape[0]].reshape(-1).astype(F32))
        at += v.shape[0]
    gain1, bias1, qb, vb, outb, gain2, bias2, downb, upb = full
    seg_own = gather_t(segment.astype(BF).reshape(1, slots), sizes).reshape(nt, slots).astype(jnp.int32)
    qb_t = mine(qb.reshape(nh, np_, ny, nx, head), (1, 3)).reshape(cols_t)
    vb_t = mine(vb.reshape(nh, np_, ny, nx, head), (1, 3)).reshape(cols_t)
    upb_t = mine(upb.reshape(nh, np_, ny, nx, nw * nc * ff_rows), (1, 3)).reshape(ff_t)

    places = jnp.arange(slots, dtype=jnp.int32)
    later = places[None, :] <= places[:, None]
    same = (seg_own[:, None, :] == 0) | (seg_own[:, None, :] == seg_own[:, :, None])
    allowed = later[None] & same & (seg_own[:, :, None] >= 0)
    allowed = allowed | (places[None, :] == places[:, None])[None]
    live = (seg_own >= 0).astype(F32)

    def to_members(w, lead, tail):
        v = w.reshape(rows, lead, nh, np_, ny, nx, tail)
        v = v.transpose(3, 5, 0, 1, 2, 4, 6).reshape(nt, rows, lead * nh * ny * tail)
        v = lax.all_to_all(v, T_AXES, 0, 0, tiled=False)
        g = lax.all_gather(v, R_AXES, axis=0)
        g = g.reshape(nh, ny, nw * nc, np_, nx, rows, lead * nh * ny * tail)
        return g.transpose(0, 3, 1, 4, 2, 5, 6).reshape(width, lead * nh * ny * tail)

    wqkv_t = to_members(w_qkv, 3, head)
    wout_t = lax.all_gather(w_out, R_AXES, axis=0).reshape(cols_t, width)
    wup_t = to_members(w_up, 1, nw * nc * ff_rows)
    wdown_t = lax.all_gather(w_down, R_AXES, axis=0).reshape(ff_t, width)

    x_all = gather_t(tokens, sizes).reshape(nt * slots, width).astype(F32)
    unit1_all, _ = ln_parts(x_all)
    n1 = (unit1_all * gain1 + bias1).astype(BF)
    proj = dot(n1, wqkv_t, ((1,), (0,)))
    q = (proj[:, :cols_t] + qb_t).astype(BF).reshape(nt, slots, heads_t, head)
    k = proj[:, cols_t : 2 * cols_t].astype(BF).reshape(nt, slots, heads_t, head)
    v = (proj[:, 2 * cols_t :] + vb_t).astype(BF).reshape(nt, slots, heads_t, head)
    scores = jnp.einsum("mqhd,mkhd->mhqk", q, k, preferred_element_type=F32) * score_scale
    scores = jnp.where(allowed[:, None], scores, F32(-1e30))
    peak = jnp.max(scores, axis=-1, keepdims=True)
    exponent = jnp.exp(scores - peak)
    probs = exponent / jnp.sum(exponent, axis=-1, keepdims=True)
    probs_low = probs.astype(BF)
    context = jnp.einsum("mhqk,mkhd->mqhd", probs_low, v, preferred_element_type=F32)
    context = (context * live[:, :, None, None]).astype(BF).reshape(nt * slots, cols_t)
    attn = scatter_t(dot(context, wout_t, ((1,), (0,))).reshape(nt, slots, width), sizes)
    inputs = tokens.astype(F32)
    residual = inputs + attn + outb

    unit2, scale2 = ln_parts(residual)
    n2 = gather_t((unit2 * gain2 + bias2).astype(BF), sizes).reshape(nt * slots, width)
    cot = gather_t(cotangent, sizes).reshape(nt * slots, width)
    up = dot(n2, wup_t, ((1,), (0,))) + upb_t
    act = gelu_tanh(up).astype(BF)
    mlp = scatter_t(dot(act, wdown_t, ((1,), (0,))).reshape(nt, slots, width), sizes)
    layer_out = (residual + mlp + downb).astype(BF)
    d_act = dot(cot, wdown_t, ((1,), (1,)))
    _, gelu_pull = jax.vjp(gelu_tanh, up)
    d_up = gelu_pull(d_act)[0].astype(BF)
    d_n2 = scatter_t(dot(d_up, wup_t, ((1,), (1,))).reshape(nt, slots, width), sizes)
    g_down = dot(act, cot, ((0,), (0,))).astype(BF)
    g_up = dot(n2, d_up, ((0,), (0,))).astype(BF)
    cot32 = cotangent.astype(F32)
    d_residual = cot32 + ln_back(d_n2, gain2, unit2, scale2)
    d_branch = d_residual.astype(BF)

    db = gather_t(d_branch, sizes).reshape(nt * slots, width)
    g_out = dot(context, db, ((0,), (0,))).astype(BF)
    d_context = dot(db, wout_t, ((1,), (1,))).reshape(nt, slots, heads_t, head)
    d_context = (d_context * live[:, :, None, None]).astype(BF)
    d_probs = jnp.einsum("mqhd,mkhd->mhqk", d_context, v, preferred_element_type=F32)
    d_v = jnp.einsum("mhqk,mqhd->mkhd", probs_low, d_context, preferred_element_type=F32)
    inner = jnp.sum(probs * d_probs, axis=-1, keepdims=True)
    d_scores = (probs * (d_probs - inner)).astype(BF)
    d_q = jnp.einsum("mhqk,mkhd->mqhd", d_scores, k, preferred_element_type=F32) * score_scale
    d_k = jnp.einsum("mhqk,mqhd->mkhd", d_scores, q, preferred_element_type=F32) * score_scale
    d_q, d_k, d_v = (u.astype(BF).reshape(nt * slots, cols_t) for u in (d_q, d_k, d_v))
    d_qkv = jnp.concatenate([d_q, d_k, d_v], axis=1)
    d_n1 = scatter_t(dot(d_qkv, wqkv_t, ((1,), (1,))).reshape(nt, slots, width), sizes)
    g_qkv = dot(n1, d_qkv, ((0,), (0,))).astype(BF)
    unit1, scale1 = ln_parts(inputs)
    tokens_grad = (d_residual + ln_back(d_n1, gain1, unit1, scale1)).astype(BF)

    def reduce_replicas(g, axis_of):
        for name in ("c", "w", "y", "h"):
            g = reduce_axis(g, axis_of[name], name, sizes)
        return g

    def from_members(g, lead, tail):
        per = lead * nh * ny * tail
        g = g.reshape(nh, np_, ny, nx, nw, nc, rows, per)
        g = reduce_replicas(g, {"c": 5, "w": 4, "y": 2, "h": 0})
        g = lax.all_to_all(g.astype(BF).reshape(nt, rows, per), T_AXES, 0, 0, tiled=False)
        g = g.reshape(np_, nx, rows, lead, nh, ny, tail).transpose(2, 3, 4, 0, 5, 1, 6)
        return g.reshape(rows, lead * nh * np_ * ny * nx * tail).astype(F32)

    w_down_grad = reduce_replicas(
        g_down.reshape(nh, ny, nw, nc, ff_rows, width), {"c": 3, "w": 2, "y": 1, "h": 0}
    )
    w_up_grad = from_members(g_up, 1, nw * nc * ff_rows)
    w_out_grad = reduce_replicas(
        g_out.reshape(nh, ny, nw, nc, rows, width), {"c": 3, "w": 2, "y": 1, "h": 0}
    )
    w_qkv_grad = from_members(g_qkv, 3, head)

    def spread(v, tail):
        v = v.reshape(nh, 1, ny, 1, tail)
        pick = (jnp.arange(np_) == pi).astype(F32).reshape(1, np_, 1, 1, 1)
        pick = pick * (jnp.arange(nx) == xi).astype(F32).reshape(1, 1, 1, nx, 1)
        return (v * pick).reshape(-1)

    terms = (
        jnp.sum(d_n1 * unit1, axis=0),
        jnp.sum(d_n1, axis=0),
        spread(jnp.sum(d_q, axis=0, dtype=F32), head),
        spread(jnp.sum(d_v, axis=0, dtype=F32), head),
        jnp.sum(d_branch, axis=0, dtype=F32),
        jnp.sum(d_n2 * unit2, axis=0),
        jnp.sum(d_n2, axis=0),
        jnp.sum(cotangent, axis=0, dtype=F32),
        spread(jnp.sum(d_up, axis=0, dtype=F32), nw * nc * ff_rows),
    )
    count = nh * np_ * ny * nx * nw * nc
    packed = jnp.concatenate([v.reshape(count, -1) for v in terms], axis=1)
    packed = lax.psum_scatter(packed, ALL, scatter_dimension=0, tiled=True)[0]
    at = 0
    outs = []
    for v in vectors:
        outs.append(packed[at : at + v.shape[0]])
        at += v.shape[0]
    g1, b1, gq, gv, go, g2, b2, gd, gu = outs
    return (
        layer_out,
        tokens_grad,
        g1,
        b1,
        w_qkv_grad,
        gq,
        gv,
        w_out_grad,
        go,
        g2,
        b2,
        w_up_grad,
        gu,
        w_down_grad,
        gd,
    )


def solution(mesh):
    dp, fsdp = mesh.shape["dp"], mesh.shape["fsdp"]
    shape = (2, 2, 2, 2, dp // 16, fsdp)
    sizes = dict(zip(ALL, shape))
    grid = Mesh(mesh.devices.reshape(shape), ALL)
    row, flat = P(ALL, None), P(ALL)
    return jax.shard_map(
        functools.partial(local, sizes),
        mesh=grid,
        in_specs=(row, row, flat, flat, row, flat, flat, row, flat, flat, row, flat, flat, flat)
        + (row, flat, row, flat),
        out_specs=(row, row, flat, flat, row, flat, flat, row, flat, flat, flat, row, flat)
        + (row, flat),
        check_vma=False,
    )
```

time: 3040 us -> 721 us (0.24)
  waiting for transfers between devices: 2540 us -> 311 us
  matrix products: 201 us -> 85.3 us
  local copies, waits for them, and re-layouts: 170 us -> 83 us
  other arithmetic: 11.5 us -> 63.3 us
  starting transfers between devices: 0.4 us -> 45.2 us
    reduce_scatter x5 -> x0, waiting for transfers between devices: 2100 us -> none  [the longest x1 705 us: local(): lax.psum_scatter(up_term, ('dp', 'fsdp'), scatter_dimension=0, tiled=True)]
    all_gather x4, waiting for transfers between devices: 441 us -> 51.3 us  [the longest x1 51.3 us: local(): wdown_t = lax.all_gather(w_down, R_AXES, axis=0).reshape(ff_t, width)]
    ppermute x0 -> x39, waiting for transfers between devices: none -> 259 us  [swap(): return lax.ppermute(x, axes, [(i, i ^ mask) for i in range(count)])]
    reshape x10 -> x16, local copies, waits for them, and re-layouts: 148 us -> 12.3 us  [the longest x4 5.64 us: to_members(): v = w.reshape(rows, lead, nh, np_, ny, nx, tail)]
    dot_general x18, matrix products: 201 us -> 85.3 us  [the longest x12 75 us: dot(): return lax.dot_general(a, b, (dims, ((), ())), preferred_element_type=F32)]
    unnamed x1 -> x0, blocking collectives: 44.6 us -> none
    all_to_all x0 -> x2, blocking collectives: none -> 41 us  [to_members(): v = lax.all_to_all(v, T_AXES, 0, 0, tiled=False)]
    ppermute x0 -> x39, starting transfers between devices: none -> 36.7 us  [swap(): return lax.ppermute(x, axes, [(i, i ^ mask) for i in range(count)])]
  transfers between devices with their start and end apart: 10 -> 46, of which waited for: 9 -> 21; matrix products, arithmetic and copies ran while one was open for 10% -> 24% of each run, Pallas kernels for 0% -> 0%
where the time goes in v1:
time: 721 us; the launch traced here: 714 us
  waiting for transfers between devices  311 us (43%)
  blocking collectives  109 us (15%)
  matrix products  85.3 us (12%)
  local copies, waits for them, and re-layouts  83 us (12%)
  other arithmetic  63.3 us (9%)
  starting transfers between devices  45.2 us (6%)
  between operations  17.1 us (2%)
    ppermute x39, waiting for transfers between devices, swap(): return lax.ppermute(x, axes, [(i, i ^ mask) for i in range(count)])  259 us
    dot_general x12, matrix products, dot(): return lax.dot_general(a, b, (dims, ((), ())), preferred_element_type=F32)  75 us
    all_gather x1, blocking collectives, local(): small_all = lax.all_gather(small, ALL, axis=0)  68 us
    all_gather x1, waiting for transfers between devices, local(): wdown_t = lax.all_gather(w_down, R_AXES, axis=0).reshape(ff_t, width)  51.3 us
    all_to_all x2, blocking collectives, to_members(): v = lax.all_to_all(v, T_AXES, 0, 0, tiled=False)  41 us
    ppermute x39, starting transfers between devices, swap(): return lax.ppermute(x, axes, [(i, i ^ mask) for i in range(count)])  36.7 us
    add x10, other arithmetic, reduce_axis(): total = total + swap(piece, (name,), m, sizes).astype(F32)  30.7 us
    convert_element_type x6, local copies, waits for them, and re-layouts, from_members(): return g.reshape(rows, lead * nh * np_ * ny * nx * tail).astype(F32)  16.8 us
  transfers between devices with their start and end apart: 46, of which 21 were waited for; matrix products, arithmetic and copies ran while one was open for 24% of the time, Pallas kernels for 0%

profile of v1, /device:TPU:0, one launch (start us, length us, event | category | flops | bytes accessed | tf_op | source)
XLA Modules:
  0.0 714.4 jit_solution(17568871866996130038)
XLA Ops:
  10.5 16.5 %all_to_all.20 = bf16[4,64,1536]{2,1,0:T(8,128)(2,1)} all-to-all(bf16[4,64,1536]{2,1,0:T(8,128)(2,1)S(1)} %reshape.732), channel_id=1, replica_groups=mesh['h'=2,'p'=2,'y'=2,'x'=2,'w'=1,'c'=2] {'p','x'}, dimensions={0} | all-to-all | bytes 1572864 | tf_op jit(solution)/shard_map/all_to_all | solution.py:144
  31.5 24.5 %all_to_all.21 = bf16[4,64,2048]{2,1,0:T(8,128)(2,1)} all-to-all(bf16[4,64,2048]{2,1,0:T(8,128)(2,1)S(1)} %reshape.742), channel_id=1, replica_groups=mesh['h'=2,'p'=2,'y'=2,'x'=2,'w'=1,'c'=2] {'p','x'}, dimensions={0} | all-to-all | bytes 2097152 | tf_op jit(solution)/shard_map/all_to_all | solution.py:144
  65.6 68.0 %all-gather.5 = bf16[32,1,896]{2,1,0:T(2,128)(2,1)S(1)} all-gather(bf16[1,1,896]{2,1,0:T(2,128)(2,1)S(1)} %reshape.792), channel_id=2, replica_groups=mesh['h'=2,'p'=2,'y'=2,'x'=2,'w'=1,'c'=2] {'h','p','y','x','w','c'}, dimensions={0}, use_global_device_ids=true | all-gather | bytes 59136 | tf_op jit(solution)/shard_map/all_gather | solution.py:122
  181.1 12.9 %collective-permute-done.8 = bf16[128,2048]{1,0:T(8,128)(2,1)S(1)} collective-permute-done((bf16[128,2048]{1,0:T(8,128)(2,1)S(1)}, bf16[128,2048]{1,0:T(8,128)(2,1)S(1)}, u32[]{:S(2)}, u32[]{:S(2)}) %collective-permute-start.8) | collective-permute-done | bytes 524320 | tf_op jit(solution)/shard_map/ppermute | solution.py:55
  194.0 18.2 %collective-permute-done.7 = bf16[128,2048]{1,0:T(8,128)(2,1)S(1)} collective-permute-done((bf16[128,2048]{1,0:T(8,128)(2,1)S(1)}, bf16[128,2048]{1,0:T(8,128)(2,1)S(1)}, u32[]{:S(2)}, u32[]{:S(2)}) %collective-permute-start.7) | collective-permute-done | bytes 524320 | tf_op jit(solution)/shard_map/ppermute | solution.py:55
  217.6 18.5 %collective-permute-done.11 = bf16[128,2048]{1,0:T(8,128)(2,1)S(1)} collective-permute-done((bf16[128,2048]{1,0:T(8,128)(2,1)S(1)}, bf16[128,2048]{1,0:T(8,128)(2,1)S(1)}, u32[]{:S(2)}, u32[]{:S(2)}) %collective-permute-start.11) | collective-permute-done | bytes 524320 | tf_op jit(solution)/shard_map/ppermute | solution.py:55
  236.0 9.3 %collective-permute-done.10 = bf16[128,2048]{1,0:T(8,128)(2,1)S(1)} collective-permute-done((bf16[128,2048]{1,0:T(8,128)(2,1)S(1)}, bf16[128,2048]{1,0:T(8,128)(2,1)S(1)}, u32[]{:S(2)}, u32[]{:S(2)}) %collective-permute-start.10) | collective-permute-done | bytes 524320 | tf_op jit(solution)/shard_map/ppermute | solution.py:55
  246.9 8.5 %copy.171 = bf16[2,2,2,2,2,64,2048]{6,5,4,3,2,1,0:T(8,128)(2,1)} copy(bf16[2,2,2,2,2,64,2048]{6,5,3,1,4,2,0:T(8,128)(2,1)} %bitcast.269) | data formatting | bytes 16777216 | tf_op jit(solution)/shard_map/transpose | solution.py:147
  255.4 9.7 %fusion.104 = f32[512,2048]{1,0:T(8,128)} fusion(bf16[512,2048]{1,0:T(8,128)(2,1)S(1)} %bitcast.293, bf16[2048,2048]{1,0:T(8,128)(2,1)} %bitcast.273), kind=kOutput, calls=%fused_computation.234 | convolution fusion | flops 4294967296 | bytes 14680064 | tf_op jit(solution)/shard_map/dot_general | solution.py:48
  265.1 51.3 %all-gather.17.cloned.1.call-done = bf16[2048,2048]{1,0:T(8,128)(2,1)} async-done(((bf16[256,2048]{1,0:T(8,128)(2,1)}), bf16[2048,2048]{1,0:T(8,128)(2,1)}) %all-gather.17.cloned.1.call-update) | async-done | bytes 8388624 | tf_op jit(solution)/shard_map/all_gather | solution.py:152
  316.4 12.2 %convert_reduce_fusion = (f32[2048]{0:T(1024)S(1)}, bf16[512,2048]{1,0:T(8,128)(2,1)S(1)}) fusion(f32[512,2048]{1,0:T(8,128)} %fusion.104, f32[2048]{0:T(1024)S(1)} %bitcast.313, bf16[512,2048]{1,0:T(8,128)(2,1)} %bitcast.290, bf16[2048,2048]{1,0:T(8,128)(2,1)} %all-gather.17.cloned.1.call-done), kind=kOutput, calls=%fused_computation.28 | convolution fusion | flops 4319082496 | bytes 16793600 | tf_op jit(solution)/shard_map/dot_general | solution.py:48
  334.9 7.2 %convolution_convert_fusion.1 = bf16[2048,2048]{1,0:T(8,128)(2,1)} fusion(bf16[512,2048]{1,0:T(8,128)(2,1)S(1)} %bitcast.294, bf16[512,2048]{1,0:T(8,128)(2,1)S(1)} %get-tuple-element.24), kind=kOutput, calls=%fused_computation.4 | convolution fusion | flops 4299161600 | bytes 12582912 | tf_op jit(solution)/shard_map/dot_general | solution.py:48
  342.1 11.0 %convolution_convert_fusion = bf16[2048,2048]{1,0:T(8,128)(2,1)} fusion(bf16[512,2048]{1,0:T(8,128)(2,1)S(1)} %bitcast.291, f32[512,2048]{1,0:T(8,128)} %fusion.104, f32[2048]{0:T(1024)S(1)} %bitcast.314), kind=kOutput, calls=%fused_computation.3 | convolution fusion | flops 4309647360 | bytes 14688256 | tf_op jit(solution)/shard_map/dot_general | solution.py:48
  357.8 9.6 %fusion.101 = (bf16[512,2048]{1,0:T(8,128)(2,1)S(1)}, f32[512,2048]{1,0:T(8,128)}) fusion(bf16[2048,2048]{1,0:T(8,128)(2,1)S(1)} %bitcast.323, f32[512,2048]{1,0:T(8,128)} %fusion.104, f32[2048]{0:T(1024)S(1)} %bitcast.315), kind=kOutput, calls=%fused_computation.231 | convolution fusion | flops 4306501632 | bytes 18882560 | tf_op jit(solution)/shard_map/dot_general | solution.py:48
  372.1 9.5 %collective-permute-done.19 = bf16[128,2048]{1,0:T(8,128)(2,1)} collective-permute-done((bf16[128,2048]{1,0:T(8,128)(2,1)}, bf16[128,2048]{1,0:T(8,128)(2,1)}, u32[]{:S(2)}, u32[]{:S(2)}) %collective-permute-start.19) | collective-permute-done | bytes 524320 | tf_op jit(solution)/shard_map/ppermute | solution.py:55
  383.8 9.0 %collective-permute-done.14 = bf16[128,2048]{1,0:T(8,128)(2,1)} collective-permute-done((bf16[128,2048]{1,0:T(8,128)(2,1)}, bf16[128,2048]{1,0:T(8,128)(2,1)}, u32[]{:S(2)}, u32[]{:S(2)}) %collective-permute-start.14) | collective-permute-done | bytes 524320 | tf_op jit(solution)/shard_map/ppermute | solution.py:55
  392.8 10.5 %collective-permute-done.13 = bf16[128,2048]{1,0:T(8,128)(2,1)} collective-permute-done((bf16[128,2048]{1,0:T(8,128)(2,1)}, bf16[128,2048]{1,0:T(8,128)(2,1)}, u32[]{:S(2)}, u32[]{:S(2)}) %collective-permute-start.13) | collective-permute-done | bytes 524320 | tf_op jit(solution)/shard_map/ppermute | solution.py:55
  422.9 10.1 %collective-permute-done.22 = bf16[128,2048]{1,0:T(8,128)(2,1)S(1)} collective-permute-done((bf16[128,2048]{1,0:T(8,128)(2,1)S(1)}, bf16[128,2048]{1,0:T(8,128)(2,1)S(1)}, u32[]{:S(2)}, u32[]{:S(2)}) %collective-permute-start.22) | collective-permute-done | bytes 524320 | tf_op jit(solution)/shard_map/ppermute | solution.py:55
  469.9 7.9 %collective-permute-done.26 = bf16[128,2048]{1,0:T(8,128)(2,1)} collective-permute-done((bf16[128,2048]{1,0:T(8,128)(2,1)}, bf16[128,2048]{1,0:T(8,128)(2,1)}, u32[]{:S(2)}, u32[]{:S(2)}) %collective-permute-start.26) | collective-permute-done | bytes 524320 | tf_op jit(solution)/shard_map/ppermute | solution.py:55
  481.2 9.9 %collective-permute-done.25 = bf16[128,2048]{1,0:T(8,128)(2,1)S(1)} collective-permute-done((bf16[128,2048]{1,0:T(8,128)(2,1)}, bf16[128,2048]{1,0:T(8,128)(2,1)S(1)}, u32[]{:S(2)}, u32[]{:S(2)}) %collective-permute-start.25) | collective-permute-done | bytes 524320 | tf_op jit(solution)/shard_map/ppermute | solution.py:55
  527.9 20.3 %collective-permute-done.28 = bf16[2,2,2,64,1536]{4,3,2,1,0:T(8,128)(2,1)} collective-permute-done((bf16[2,2,2,64,1536]{4,3,2,1,0:T(8,128)(2,1)}, bf16[2,2,2,64,1536]{4,3,2,1,0:T(8,128)(2,1)}, u32[]{:S(2)}, u32[]{:S(2)}) %collective-permute-start.28) | collective-permute-done | bytes 1572896 | tf_op jit(solution)/shard_map/ppermute | solution.py:55
  551.4 41.9 %collective-permute-done.34 = bf16[2,2,2,64,2048]{4,3,2,1,0:T(8,128)(2,1)} collective-permute-done((bf16[2,2,2,64,2048]{4,3,2,1,0:T(8,128)(2,1)}, bf16[2,2,2,64,2048]{4,3,2,1,0:T(8,128)(2,1)}, u32[]{:S(2)}, u32[]{:S(2)}) %collective-permute-start.34) | collective-permute-done | bytes 2097184 | tf_op jit(solution)/shard_map/ppermute | solution.py:55
  603.9 31.1 %collective-permute-done.37 = bf16[2,256,2048]{2,1,0:T(8,128)(2,1)} collective-permute-done((bf16[2,256,2048]{2,1,0:T(8,128)(2,1)}, bf16[2,256,2048]{2,1,0:T(8,128)(2,1)}, u32[]{:S(2)}, u32[]{:S(2)}) %collective-permute-start.37) | collective-permute-done | bytes 2097184 | tf_op jit(solution)/shard_map/ppermute | solution.py:55
  654.9 32.2 %collective-permute-done.38 = bf16[256,2048]{1,0:T(8,128)(2,1)} collective-permute-done((bf16[256,2048]{1,0:T(8,128)(2,1)}, bf16[256,2048]{1,0:T(8,128)(2,1)}, u32[]{:S(2)}, u32[]{:S(2)}) %collective-permute-start.38) | collective-permute-done | bytes 1048608 | tf_op jit(solution)/shard_map/ppermute | solution.py:55
  (319 shorter events, 237.5 us)
Async XLA Ops:
  7.2 137.1 %all-gather.11.cloned.1.call-start = ((), (), s32[]{:S(2)}) async-start(), calls=%async_computation.4 | async-start | bytes 7077888 | tf_op jit(solution)/shard_map/all_gather | solution.py:145
  27.0 139.2 %all-gather.13.cloned.1.call-start = ((), (), s32[]{:S(2)}) async-start(), calls=%async_computation.5 | async-start | bytes 2359296 | tf_op jit(solution)/shard_map/all_gather | solution.py:150
  27.8 219.1 %all-gather.15.cloned.1.call-start = ((), (), s32[]{:S(2)}) async-start(), calls=%async_computation.6 | async-start | bytes 9437184 | tf_op jit(solution)/shard_map/all_gather | solution.py:145
  56.0 260.4 %all-gather.17.cloned.1.call-start = ((), (), s32[]{:S(2)}) async-start(), calls=%async_computation.7 | async-start | bytes 9437184 | tf_op jit(solution)/shard_map/all_gather | solution.py:152
  56.6 593.5 %all-reduce.3.cloned.1.call-start = ((), (), s32[]{:S(2)}) async-start(), calls=%async_computation.8 | async-start | bytes 196608
  59.5 75.2 %collective-permute-start.5 = (bf16[1,128]{1,0:T(2,128)(2,1)S(1)}, bf16[1,128]{1,0:T(2,128)(2,1)S(1)}, u32[]{:S(2)}, u32[]{:S(2)}) collective-permute-start(bf16[1,128]{1,0:T(2,128)(2,1)S(1)} %fusion.82), channel_id=1, source_target_pairs={{0,10},{2,8},{8,2},{10,0},{1,11},{3,9},{9,3},{11,1},{4,14},{6,12},... | collective-permute-start | bytes 776 | tf_op jit(solution)/shard_map/ppermute | solution.py:55
  60.4 76.8 %collective-permute-start.4 = (bf16[1,128]{1,0:T(2,128)(2,1)S(1)}, bf16[1,128]{1,0:T(2,128)(2,1)S(1)}, u32[]{:S(2)}, u32[]{:S(2)}) collective-permute-start(bf16[1,128]{1,0:T(2,128)(2,1)S(1)} %fusion.82), channel_id=1, source_target_pairs={{0,8},{2,10},{8,0},{10,2},{1,9},{3,11},{9,1},{11,3},{4,12},{6,14},... | collective-permute-start | bytes 776 | tf_op jit(solution)/shard_map/ppermute | solution.py:55
  61.9 77.1 %collective-permute-start.2 = (bf16[128,2048]{1,0:T(8,128)(2,1)S(1)}, bf16[128,2048]{1,0:T(8,128)(2,1)S(1)}, u32[]{:S(2)}, u32[]{:S(2)}) collective-permute-start(bf16[128,2048]{1,0:T(8,128)(2,1)S(1)} %copy-done), channel_id=1, source_target_pairs={{0,10},{2,8},{8,2},{10,0},{1,11},{3,9},{9,3},{11,1},{4,14},{6,12},... | collective-permute-start | bytes 1572872 | tf_op jit(solution)/shard_map/ppermute | solution.py:55
  63.0 78.1 %collective-permute-start.1 = (bf16[128,2048]{1,0:T(8,128)(2,1)S(1)}, bf16[128,2048]{1,0:T(8,128)(2,1)S(1)}, u32[]{:S(2)}, u32[]{:S(2)}) collective-permute-start(bf16[128,2048]{1,0:T(8,128)(2,1)S(1)} %copy-done), channel_id=1, source_target_pairs={{0,8},{2,10},{8,0},{10,2},{1,9},{3,11},{9,1},{11,3},{4,12},{6,14},... | collective-permute-start | bytes 1572872 | tf_op jit(solution)/shard_map/ppermute | solution.py:55
  64.5 76.6 %collective-permute-start = (bf16[128,2048]{1,0:T(8,128)(2,1)S(1)}, bf16[128,2048]{1,0:T(8,128)(2,1)S(1)}, u32[]{:S(2)}, u32[]{:S(2)}) collective-permute-start(bf16[128,2048]{1,0:T(8,128)(2,1)S(1)} %copy-done), channel_id=1, source_target_pairs={{0,2},{2,0},{8,10},{10,8},{1,3},{3,1},{9,11},{11,9},{4,6},{6,4},{1... | collective-permute-start | bytes 1572872 | tf_op jit(solution)/shard_map/ppermute | solution.py:55
  170.8 41.3 %collective-permute-start.7 = (bf16[128,2048]{1,0:T(8,128)(2,1)S(1)}, bf16[128,2048]{1,0:T(8,128)(2,1)S(1)}, u32[]{:S(2)}, u32[]{:S(2)}) collective-permute-start(bf16[128,2048]{1,0:T(8,128)(2,1)S(1)} %get-tuple-element.54), channel_id=1, source_target_pairs={{0,8},{2,10},{8,0},{10,2},{1,9},{3,11},{9,1},{11,3},{4,12},{6,14},... | collective-permute-start | bytes 1572872 | tf_op jit(solution)/shard_map/ppermute | solution.py:55
  171.5 40.7 %collective-permute-start.6 = (bf16[128,2048]{1,0:T(8,128)(2,1)S(1)}, bf16[128,2048]{1,0:T(8,128)(2,1)S(1)}, u32[]{:S(2)}, u32[]{:S(2)}) collective-permute-start(bf16[128,2048]{1,0:T(8,128)(2,1)S(1)} %get-tuple-element.52), channel_id=1, source_target_pairs={{0,2},{2,0},{8,10},{10,8},{1,3},{3,1},{9,11},{11,9},{4,6},{6,4},{1... | collective-permute-start | bytes 1572872 | tf_op jit(solution)/shard_map/ppermute | solution.py:55
  415.8 96.3 %collective-permute-start.33 = (bf16[2,2,2,2,1,64,2048]{6,5,3,2,1,0,4:T(8,128)(2,1)}, bf16[2,2,2,2,1,64,2048]{6,5,3,2,1,0,4:T(8,128)(2,1)}, u32[]{:S(2)}, u32[]{:S(2)}) collective-permute-start(bf16[2,2,2,2,1,64,2048]{6,5,3,2,1,0,4:T(8,128)(2,1)} %dynamic-slice_bitcast_fusion), channel_id=1, source_target_pairs={{0,1},{1,0},{2,3},{3,2},{4,5},{5,4},{6,7},{7,6},{8,9},{9,8},{10,11... | collective-permute-start | bytes 12582920 | tf_op jit(solution)/shard_map/ppermute | solution.py:55
  458.4 46.3 %collective-permute-start.27 = (bf16[2,2,2,2,1,64,1536]{6,5,3,2,1,0,4:T(8,128)(2,1)}, bf16[2,2,2,2,1,64,1536]{6,5,3,2,1,0,4:T(8,128)(2,1)}, u32[]{:S(2)}, u32[]{:S(2)}) collective-permute-start(bf16[2,2,2,2,1,64,1536]{6,5,3,2,1,0,4:T(8,128)(2,1)} %dynamic-slice_bitcast_fusion.1), channel_id=1, source_target_pairs={{0,1},{1,0},{2,3},{3,2},{4,5},{5,4},{6,7},{7,6},{8,9},{9,8},{10,11... | collective-permute-start | bytes 9437192 | tf_op jit(solution)/shard_map/ppermute | solution.py:55
  469.3 52.3 %collective-permute-start.36 = (bf16[2,2,1,256,2048]{4,3,0,2,1:T(8,128)(2,1)}, bf16[2,2,1,256,2048]{4,3,0,2,1:T(8,128)(2,1)}, u32[]{:S(2)}, u32[]{:S(2)}) collective-permute-start(bf16[2,2,1,256,2048]{4,3,0,2,1:T(8,128)(2,1)} %bitcast.239), channel_id=1, source_target_pairs={{0,1},{1,0},{2,3},{3,2},{4,5},{5,4},{6,7},{7,6},{8,9},{9,8},{10,11... | collective-permute-start | bytes 12582920 | tf_op jit(solution)/shard_map/ppermute | solution.py:55
  510.5 37.8 %collective-permute-start.28 = (bf16[2,2,2,64,1536]{4,3,2,1,0:T(8,128)(2,1)}, bf16[2,2,2,64,1536]{4,3,2,1,0:T(8,128)(2,1)}, u32[]{:S(2)}, u32[]{:S(2)}) collective-permute-start(bf16[2,2,2,64,1536]{4,3,2,1,0:T(8,128)(2,1)} %fusion.17), channel_id=1, source_target_pairs={{0,4},{4,0},{1,5},{5,1},{2,6},{6,2},{3,7},{7,3},{8,12},{12,8},{9,1... | collective-permute-start | bytes 4718600 | tf_op jit(solution)/shard_map/ppermute | solution.py:55
  519.2 74.2 %collective-permute-start.34 = (bf16[2,2,2,64,2048]{4,3,2,1,0:T(8,128)(2,1)}, bf16[2,2,2,64,2048]{4,3,2,1,0:T(8,128)(2,1)}, u32[]{:S(2)}, u32[]{:S(2)}) collective-permute-start(bf16[2,2,2,64,2048]{4,3,2,1,0:T(8,128)(2,1)} %fusion.12), channel_id=1, source_target_pairs={{0,4},{4,0},{1,5},{5,1},{2,6},{6,2},{3,7},{7,3},{8,12},{12,8},{9,1... | collective-permute-start | bytes 6291464 | tf_op jit(solution)/shard_map/ppermute | solution.py:55
  521.3 131.6 %collective-permute-start.32 = (bf16[64,2048]{1,0:T(8,128)(2,1)}, bf16[64,2048]{1,0:T(8,128)(2,1)}, u32[]{:S(2)}, u32[]{:S(2)}) collective-permute-start(bf16[64,2048]{1,0:T(8,128)(2,1)} %fusion.75), channel_id=1, source_target_pairs={{0,16},{16,0},{1,17},{17,1},{2,18},{18,2},{3,19},{19,3},{4,20},{20... | collective-permute-start | bytes 786440 | tf_op jit(solution)/shard_map/ppermute | solution.py:55
  527.5 107.6 %collective-permute-start.37 = (bf16[2,256,2048]{2,1,0:T(8,128)(2,1)}, bf16[2,256,2048]{2,1,0:T(8,128)(2,1)}, u32[]{:S(2)}, u32[]{:S(2)}) collective-permute-start(bf16[2,256,2048]{2,1,0:T(8,128)(2,1)} %fusion.13), channel_id=1, source_target_pairs={{0,4},{4,0},{1,5},{5,1},{2,6},{6,2},{3,7},{7,3},{8,12},{12,8},{9,1... | collective-permute-start | bytes 6291464 | tf_op jit(solution)/shard_map/ppermute | solution.py:55
  551.2 47.6 %collective-permute-start.29 = (bf16[2,2,64,1536]{3,2,1,0:T(8,128)(2,1)S(1)}, bf16[2,2,64,1536]{3,2,1,0:T(8,128)(2,1)S(1)}, u32[]{:S(2)}, u32[]{:S(2)}) collective-permute-start(bf16[2,2,64,1536]{3,2,1,0:T(8,128)(2,1)S(1)} %fusion.63), channel_id=1, source_target_pairs={{0,16},{16,0},{1,17},{17,1},{2,18},{18,2},{3,19},{19,3},{4,20},{20... | collective-permute-start | bytes 2359304 | tf_op jit(solution)/shard_map/ppermute | solution.py:55
  598.6 43.3 %collective-permute-start.35 = (bf16[2,2,64,2048]{3,2,1,0:T(8,128)(2,1)}, bf16[2,2,64,2048]{3,2,1,0:T(8,128)(2,1)}, u32[]{:S(2)}, u32[]{:S(2)}) collective-permute-start(bf16[2,2,64,2048]{3,2,1,0:T(8,128)(2,1)} %fusion.48), channel_id=1, source_target_pairs={{0,16},{16,0},{1,17},{17,1},{2,18},{18,2},{3,19},{19,3},{4,20},{20... | collective-permute-start | bytes 3145736 | tf_op jit(solution)/shard_map/ppermute | solution.py:55
  599.9 44.6 %all-to-all-start.2 = ((bf16[4,64,1536]{2,1,0:T(8,128)(2,1)}), bf16[4,64,1536]{2,1,0:T(8,128)(2,1)S(1)}, u32[]{:S(2)}, u32[]{:S(2)}) async-start(bf16[4,64,1536]{2,1,0:T(8,128)(2,1)} %bitcast.67), calls=%async_computation.2 | async-start | bytes 1572864 | tf_op jit(solution)/shard_map/all_to_all | solution.py:216
  641.6 45.4 %collective-permute-start.38 = (bf16[256,2048]{1,0:T(8,128)(2,1)}, bf16[256,2048]{1,0:T(8,128)(2,1)}, u32[]{:S(2)}, u32[]{:S(2)}) collective-permute-start(bf16[256,2048]{1,0:T(8,128)(2,1)} %fusion.49), channel_id=1, source_target_pairs={{0,16},{16,0},{1,17},{17,1},{2,18},{18,2},{3,19},{19,3},{4,20},{20... | collective-permute-start | bytes 3145736 | tf_op jit(solution)/shard_map/ppermute | solution.py:55
  644.5 52.9 %all-to-all-start.3 = ((bf16[4,64,2048]{2,1,0:T(8,128)(2,1)}), bf16[4,64,2048]{2,1,0:T(8,128)(2,1)}, u32[]{:S(2)}, u32[]{:S(2)}) async-start(bf16[4,64,2048]{2,1,0:T(8,128)(2,1)} %bitcast.89), calls=%async_computation.3 | async-start | bytes 2097152 | tf_op jit(solution)/shard_map/all_to_all | solution.py:216
  (68 other events, 1195.7 us)
Sparse Core Ops, SparseCore 0:
  27.2 71.5 all-gather.10
  100.6 36.2 all-gather.12
  138.8 87.9 all-gather.14
  228.5 87.8 all-gather.16
  496.4 149.6 all-reduce.2

commit v2 on v1

--- a/solution.py
+++ b/solution.py
@@ -3,6 +3,8 @@
 import jax
 import jax.numpy as jnp
 from jax import lax
+from jax.experimental import pallas as pl
+from jax.experimental.pallas import tpu as pltpu
 from jax.sharding import Mesh
 from jax.sharding import PartitionSpec as P
 
@@ -13,6 +15,241 @@
 T_AXES = ("p", "x")
 R_AXES = ("h", "y", "w", "c")
 ALL = ("h", "p", "y", "x", "w", "c")
+
+MESH_ID = pl.DeviceIdType.MESH
+
+
+class Wire:
+    def __init__(self, sizes, send, recv, local, bounce):
+        self.sizes = sizes
+        self.send, self.recv, self.local, self.bounce = send, recv, local, bounce
+        self.at = {name: lax.axis_index(name) for name in ALL}
+        self.count = 0
+        self.kept = 0
+        self.sent = []
+
+    def greet(self, axes):
+        barrier = pltpu.get_barrier_semaphore()
+        peers = []
+        if "t" in axes:
+            peers += [self.member(m) for m in (1, 2, 3)]
+        for name in axes:
+            if name != "t":
+                peers += self.others(name)
+        for peer in peers:
+            pl.semaphore_signal(barrier, inc=1, device_id=peer, device_id_type=MESH_ID)
+        pl.semaphore_wait(barrier, len(peers))
+
+    def member(self, m):
+        peer = {}
+        if m & 2:
+            peer["p"] = 1 - self.at["p"]
+        if m & 1:
+            peer["x"] = 1 - self.at["x"]
+        return peer
+
+    def others(self, name):
+        count = self.sizes[name]
+        return [{name: lax.rem(self.at[name] + k, count)} for k in range(1, count)]
+
+    def put(self, source, target, peer):
+        copy = pltpu.make_async_remote_copy(
+            src_ref=source,
+            dst_ref=target,
+            send_sem=self.send.at[self.count],
+            recv_sem=self.recv.at[self.count],
+            device_id=peer,
+            device_id_type=MESH_ID,
+        )
+        self.count += 1
+        copy.start()
+        self.sent.append(copy)
+        return copy
+
+    def where(self, dims, free):
+        return tuple(slice(None) if d in free else self.at[d] for d in dims)
+
+    def spread(self, ref, dims, free, name, source=None, tail=()):
+        place = ref.at[self.where(dims, free) + tail]
+        return [
+            self.put(place if source is None else source, place, peer)
+            for peer in self.others(name)
+        ]
+
+    def keep(self, source, target):
+        room = self.bounce[self.kept]
+        sem = self.local.at[self.kept]
+        self.kept += 1
+        first = pltpu.make_async_copy(source, room, sem)
+        first.start()
+        second = pltpu.make_async_copy(room, target, sem)
+
+        def go():
+            first.wait()
+            second.start()
+            return second
+
+        return go
+
+    def close(self):
+        for copy in self.sent:
+            copy.wait_send()
+
+
+def arrive(copies):
+    for copy in copies:
+        copy.wait_recv()
+
+
+def comm_call(name, cid, sizes, body, ins, outs, bounce=(), scratch=(), copies=64):
+    nb = len(bounce)
+
+    def kernel(*refs):
+        n_in, n_out = len(ins), len(outs)
+        in_refs, out_refs = refs[:n_in], refs[n_in : n_in + n_out]
+        rest = refs[n_in + n_out :]
+        send, recv, local = rest[:3]
+        wire = Wire(sizes, send, recv, local, rest[3 : 3 + nb])
+        body(wire, in_refs, out_refs, rest[3 + nb :])
+        wire.close()
+
+    return pl.pallas_call(
+        kernel,
+        out_shape=outs,
+        in_specs=[pl.BlockSpec(memory_space=pl.ANY)] * len(ins),
+        out_specs=[pl.BlockSpec(memory_space=pl.ANY)] * len(outs),
+        scratch_shapes=[
+            pltpu.SemaphoreType.DMA((copies,)),
+            pltpu.SemaphoreType.DMA((copies,)),
+            pltpu.SemaphoreType.DMA((max(nb, 1),)),
+        ]
+        + [pltpu.VMEM(s, BF) for s in bounce]
+        + list(scratch),
+        compiler_params=pltpu.CompilerParams(
+            collective_id=cid, has_side_effects=True, vmem_limit_bytes=60000 * 1024
+        ),
+        name=name,
+    )(*ins)
+
+
+MEMBER = "hpyxwc"
+STRIPE = "hywc"
+
+
+def gather_first(wire, ins, outs, _):
+    tok, sm, wo, wqkv = ins[0], ins[1], ins[2], ins[3:]
+    X, S, O, W = outs[0], outs[1], outs[2], outs[3:]
+    at = wire.at
+    own = wire.where(MEMBER, "")
+    goes = [wire.keep(sm, S.at[own])]
+    goes += [wire.keep(wqkv[i].at[at["p"], at["x"]], W[i].at[own]) for i in range(3)]
+    goes += [wire.keep(wo, O.at[wire.where(STRIPE, "")])]
+    goes += [wire.keep(tok, X.at[0])]
+    wire.greet(("t", "h", "y", "c", "w"))
+    s_in = [wire.put(sm, S.at[own], wire.member(m)) for m in (1, 2, 3)]
+    w_in = []
+    for i in range(3):
+        part = []
+        for m in (1, 2, 3):
+            peer = wire.member(m)
+            src = wqkv[i].at[peer.get("p", at["p"]), peer.get("x", at["x"])]
+            part.append(wire.put(src, W[i].at[own], peer))
+        w_in.append(part)
+    o_in = wire.spread(O, STRIPE, "", "h", source=wo)
+    x_in = [wire.put(tok, X.at[m], wire.member(m)) for m in (1, 2, 3)]
+    held = [go() for go in goes]
+    held[0].wait()
+    arrive(s_in)
+    s_in = wire.spread(S, MEMBER, "px", "h")
+    for i in range(3):
+        held[1 + i].wait()
+        arrive(w_in[i])
+        w_in[i] = wire.spread(W[i], MEMBER, "px", "h")
+    held[4].wait()
+    arrive(o_in)
+    o_in = wire.spread(O, STRIPE, "h", "y")
+    arrive(s_in)
+    s_in = wire.spread(S, MEMBER, "hpx", "y")
+    for i in range(3):
+        arrive(w_in[i])
+        w_in[i] = wire.spread(W[i], MEMBER, "hpx", "y")
+        if i == 0:
+            arrive(s_in)
+            s_in = wire.spread(S, MEMBER, "hpyx", "c")
+            arrive(o_in)
+            o_in = wire.spread(O, STRIPE, "hy", "c")
+    for i in range(3):
+        arrive(w_in[i])
+        w_in[i] = wire.spread(W[i], MEMBER, "hpyx", "c")
+    for stream, ref, dims, free in [(s_in, S, MEMBER, "hpyxc"), (o_in, O, STRIPE, "hyc")] + [
+        (w_in[i], W[i], MEMBER, "hpyxc") for i in range(3)
+    ]:
+        arrive(stream)
+        arrive(wire.spread(ref, dims, free, "w"))
+    held[5].wait()
+    arrive(x_in)
+
+
+def gather_second(chunks, wire, ins, outs, _):
+    parts, wd, wu = ins
+    R, D, U = outs
+    at = wire.at
+    own = wire.where(STRIPE, "")
+    goes = [wire.keep(wd, D.at[own]), wire.keep(wu.at[at["p"], at["x"]], U.at[at["p"], at["x"]])]
+    wire.greet(("t", "h", "y", "c", "w"))
+    r_in = [wire.put(parts.at[m], R.at[m - 1], wire.member(m)) for m in (1, 2, 3)]
+    rows = wd.shape[0] // chunks
+    cut = [(pl.ds(i * rows, rows),) for i in range(chunks)]
+    d_in = [
+        wire.spread(D, STRIPE, "", "h", source=wd.at[cut[i]], tail=cut[i]) for i in range(chunks)
+    ]
+    u_in = []
+    for m in (1, 2, 3):
+        peer = wire.member(m)
+        src = wu.at[peer.get("p", at["p"]), peer.get("x", at["x"])]
+        u_in.append(wire.put(src, U.at[at["p"], at["x"]], peer))
+    held = [go() for go in goes]
+    held[0].wait()
+    held[1].wait()
+    for name, free in (("y", "h"), ("c", "hy"), ("w", "hyc")):
+        for i in range(chunks):
+            arrive(d_in[i])
+            d_in[i] = wire.spread(D, STRIPE, free, name, tail=cut[i])
+    for i in range(chunks):
+        arrive(d_in[i])
+    arrive(u_in)
+    arrive(r_in)
+
+
+def gather_third(chunks, wire, ins, outs, _):
+    n2, cot, wu = ins
+    N, C, U = outs
+    own = wire.where(MEMBER, "px")
+    goes = [wire.keep(wu, U.at[own]), wire.keep(n2, N.at[0]), wire.keep(cot, C.at[0])]
+    wire.greet(("t", "h", "y", "c", "w"))
+    n_in = [wire.put(n2, N.at[m], wire.member(m)) for m in (1, 2, 3)]
+    rows = wu.shape[2] // chunks
+    every = (slice(None),) * 2
+    cut = [(pl.ds(i * rows, rows),) for i in range(chunks)]
+    u_in = [
+        wire.spread(U, MEMBER, "px", "h", source=wu.at[every + cut[i]], tail=cut[i])
+        for i in range(chunks)
+    ]
+    n_in += [wire.put(cot, C.at[m], wire.member(m)) for m in (1, 2, 3)]
+    held = [go() for go in goes]
+    for h in held:
+        h.wait()
+    for name, free in (("y", "hpx"), ("c", "hpyx"), ("w", "hpyxc")):
+        for i in range(chunks):
+            arrive(u_in[i])
+            u_in[i] = wire.spread(U, MEMBER, free, name, tail=cut[i])
+    for i in range(chunks):
+        arrive(u_in[i])
+    arrive(n_in)
+
+
+def shape_of(*dims):
+    return jax.ShapeDtypeStruct(dims, BF)
 
 
 def ln_parts(values_in):
@@ -119,14 +356,44 @@
     unit = hidden // width
     vectors = (ln1_gain, ln1_bias, q_bias, v_bias, out_bias, ln2_gain, ln2_bias, down_bias, up_bias)
     small = jnp.concatenate(vectors + (segment.astype(BF),))
-    small_all = lax.all_gather(small, ALL, axis=0)
+    lead = (nh, np_, ny, nx, nw, nc)
+    small = jnp.pad(small, (0, 1024 - small.shape[0])).reshape(8, 128)
+    wq = w_qkv.reshape(rows, 3, nh, np_, ny, nx, head).transpose(1, 3, 5, 0, 2, 4, 6)
+    wq = wq.reshape(3, np_, nx, rows, cols_t)
+    wu = w_up.reshape(rows, nh, np_, ny, nx, nw * nc * ff_rows).transpose(2, 4, 0, 1, 3, 5)
+    wu = wu.reshape(np_, nx, rows, ff_t)
+    x_all, small_all, wout_t, wq_t, wk_t, wv_t = comm_call(
+        "gather_first",
+        1,
+        sizes,
+        gather_first,
+        (tokens, small, w_out, wq[0], wq[1], wq[2]),
+        (
+            shape_of(nt, slots, width),
+            shape_of(*lead, 8, 128),
+            shape_of(nh, ny, nw, nc, rows, width),
+        )
+        + (shape_of(*lead, rows, cols_t),) * 3,
+        bounce=((8, 128),) + ((rows, cols_t),) * 3 + ((rows, width), (slots, width)),
+    )
+    wout_t = wout_t.reshape(cols_t, width)
+    wq_t, wk_t, wv_t = (u.reshape(width, cols_t) for u in (wq_t, wk_t, wv_t))
+    small_own = lax.dynamic_slice(
+        small_all.reshape(nh, np_, ny, nx, nw, nc, 1024),
+        tuple(lax.axis_index(a) if a not in T_AXES else 0 for a in ALL) + (0,),
+        (1, np_, 1, nx, 1, 1, 1024),
+    ).reshape(nt, 1024)
+    small_all = small_all.reshape(-1, 1024)
     at = 0
     full = []
     for v in vectors:
         full.append(small_all[:, at : at + v.shape[0]].reshape(-1).astype(F32))
         at += v.shape[0]
     gain1, bias1, qb, vb, outb, gain2, bias2, downb, upb = full
-    seg_own = gather_t(segment.astype(BF).reshape(1, slots), sizes).reshape(nt, slots).astype(jnp.int32)
+    seg_own = small_own[:, at : at + slots]
+    seg_own = jnp.where(xi == 0, seg_own, seg_own.reshape(2, 2, slots)[:, ::-1].reshape(4, slots))
+    seg_own = jnp.where(pi == 0, seg_own, seg_own.reshape(2, 2, slots)[::-1].reshape(4, slots))
+    seg_own = seg_own.astype(jnp.int32)
     qb_t = mine(qb.reshape(nh, np_, ny, nx, head), (1, 3)).reshape(cols_t)
     vb_t = mine(vb.reshape(nh, np_, ny, nx, head), (1, 3)).reshape(cols_t)
     upb_t = mine(upb.reshape(nh, np_, ny, nx, nw * nc * ff_rows), (1, 3)).reshape(ff_t)
@@ -138,26 +405,12 @@
     allowed = allowed | (places[None, :] == places[:, None])[None]
     live = (seg_own >= 0).astype(F32)
 
-    def to_members(w, lead, tail):
-        v = w.reshape(rows, lead, nh, np_, ny, nx, tail)
-        v = v.transpose(3, 5, 0, 1, 2, 4, 6).reshape(nt, rows, lead * nh * ny * tail)
-        v = lax.all_to_all(v, T_AXES, 0, 0, tiled=False)
-        g = lax.all_gather(v, R_AXES, axis=0)
-        g = g.reshape(nh, ny, nw * nc, np_, nx, rows, lead * nh * ny * tail)
-        return g.transpose(0, 3, 1, 4, 2, 5, 6).reshape(width, lead * nh * ny * tail)
-
-    wqkv_t = to_members(w_qkv, 3, head)
-    wout_t = lax.all_gather(w_out, R_AXES, axis=0).reshape(cols_t, width)
-    wup_t = to_members(w_up, 1, nw * nc * ff_rows)
-    wdown_t = lax.all_gather(w_down, R_AXES, axis=0).reshape(ff_t, width)
-
-    x_all = gather_t(tokens, sizes).reshape(nt * slots, width).astype(F32)
+    x_all = x_all.reshape(nt * slots, width).astype(F32)
     unit1_all, _ = ln_parts(x_all)
     n1 = (unit1_all * gain1 + bias1).astype(BF)
-    proj = dot(n1, wqkv_t, ((1,), (0,)))
-    q = (proj[:, :cols_t] + qb_t).astype(BF).reshape(nt, slots, heads_t, head)
-    k = proj[:, cols_t : 2 * cols_t].astype(BF).reshape(nt, slots, heads_t, head)
-    v = (proj[:, 2 * cols_t :] + vb_t).astype(BF).reshape(nt, slots, heads_t, head)
+    q = (dot(n1, wq_t, ((1,), (0,))) + qb_t).astype(BF).reshape(nt, slots, heads_t, head)
+    k = dot(n1, wk_t, ((1,), (0,))).astype(BF).reshape(nt, slots, heads_t, head)
+    v = (dot(n1, wv_t, ((1,), (0,))) + vb_t).astype(BF).reshape(nt, slots, heads_t, head)
     scores = jnp.einsum("mqhd,mkhd->mhqk", q, k, preferred_element_type=F32) * score_scale
     scores = jnp.where(allowed[:, None], scores, F32(-1e30))
     peak = jnp.max(scores, axis=-1, keepdims=True)
@@ -166,13 +419,40 @@
     probs_low = probs.astype(BF)
     context = jnp.einsum("mhqk,mkhd->mqhd", probs_low, v, preferred_element_type=F32)
     context = (context * live[:, :, None, None]).astype(BF).reshape(nt * slots, cols_t)
-    attn = scatter_t(dot(context, wout_t, ((1,), (0,))).reshape(nt, slots, width), sizes)
+    part = dot(context, wout_t, ((1,), (0,))).reshape(nt, slots, width)
+    others, wdown_t, wu = comm_call(
+        "gather_second",
+        2,
+        sizes,
+        functools.partial(gather_second, 4),
+        (part.astype(BF), w_down, wu),
+        (
+            shape_of(nt - 1, slots, width),
+            shape_of(nh, ny, nw, nc, ff_rows, width),
+            shape_of(np_, nx, rows, ff_t),
+        ),
+        bounce=((ff_rows, width), (rows, ff_t)),
+    )
+    wdown_t = wdown_t.reshape(ff_t, width)
     inputs = tokens.astype(F32)
-    residual = inputs + attn + outb
+    residual = inputs + part[0] + jnp.sum(others.astype(F32), axis=0) + outb
 
     unit2, scale2 = ln_parts(residual)
-    n2 = gather_t((unit2 * gain2 + bias2).astype(BF), sizes).reshape(nt * slots, width)
-    cot = gather_t(cotangent, sizes).reshape(nt * slots, width)
+    n2, cot, wup_t = comm_call(
+        "gather_third",
+        3,
+        sizes,
+        functools.partial(gather_third, 4 if rows % 64 == 0 else 1),
+        ((unit2 * gain2 + bias2).astype(BF), cotangent, wu),
+        (
+            shape_of(nt, slots, width),
+            shape_of(nt, slots, width),
+            shape_of(*lead, rows, ff_t),
+        ),
+        bounce=((np_, nx, rows, ff_t), (slots, width), (slots, width)),
+    )
+    n2, cot = n2.reshape(nt * slots, width), cot.reshape(nt * slots, width)
+    wup_t = wup_t.reshape(width, ff_t)
     up = dot(n2, wup_t, ((1,), (0,))) + upb_t
     act = gelu_tanh(up).astype(BF)
     mlp = scatter_t(dot(act, wdown_t, ((1,), (0,))).reshape(nt, slots, width), sizes)
@@ -199,7 +479,8 @@
     d_k = jnp.einsum("mhqk,mqhd->mkhd", d_scores, q, preferred_element_type=F32) * score_scale
     d_q, d_k, d_v = (u.astype(BF).reshape(nt * slots, cols_t) for u in (d_q, d_k, d_v))
     d_qkv = jnp.concatenate([d_q, d_k, d_v], axis=1)
-    d_n1 = scatter_t(dot(d_qkv, wqkv_t, ((1,), (1,))).reshape(nt, slots, width), sizes)
+    d_n1 = dot(d_q, wq_t, ((1,), (1,))) + dot(d_k, wk_t, ((1,), (1,))) + dot(d_v, wv_t, ((1,), (1,)))
+    d_n1 = scatter_t(d_n1.reshape(nt, slots, width), sizes)
     g_qkv = dot(n1, d_qkv, ((0,), (0,))).astype(BF)
     unit1, scale1 = ln_parts(inputs)
     tokens_grad = (d_residual + ln_back(d_n1, gain1, unit1, scale1)).astype(BF)

time: 721 us -> 737 us (1.022)
  Pallas kernels: 0 us -> 245 us
  waiting for transfers between devices: 311 us -> 183 us
  blocking collectives: 109 us -> 0 us
  matrix products: 85.3 us -> 96.3 us
    pallas_call x0 -> x3, Pallas kernels: none -> 245 us  [comm_call(): pl.pallas_call(kernel, out_shape=outs, in_specs=[pl.BlockSpec(memory_spac...]
    ppermute x39 -> x24, waiting for transfers between devices: 259 us -> 163 us  [swap(): return lax.ppermute(x, axes, [(i, i ^ mask) for i in range(count)])]
    all_gather x1 -> x0, blocking collectives: 68 us -> none  [local(): small_all = lax.all_gather(small, ALL, axis=0)]
    all_gather x4 -> x0, waiting for transfers between devices: 51.3 us -> none  [the longest x1 51.3 us: local(): wdown_t = lax.all_gather(w_down, R_AXES, axis=0).reshape(ff_t, width)]
    all_to_all x2 -> x0, blocking collectives: 41 us -> none  [to_members(): v = lax.all_to_all(v, T_AXES, 0, 0, tiled=False)]
    unnamed x6 -> x2, waiting for transfers between devices: 1.27 us -> 19.8 us
    transpose x2 -> x0, local copies, waits for them, and re-layouts: 12.8 us -> none  [to_members(): g.transpose(0, 3, 1, 4, 2, 5, 6).reshape(width, lead * nh * ny * tail)]
    dot_general x12 -> x16, matrix products: 75 us -> 87 us  [dot(): return lax.dot_general(a, b, (dims, ((), ())), preferred_element_type=F32)]
  transfers between devices with their start and end apart: 46 -> 27, of which waited for: 21 -> 12; matrix products, arithmetic and copies ran while one was open for 24% -> 20% of each run, Pallas kernels for 0% -> 0%
where the time goes in v2:
time: 737 us; the launch traced here: 728 us
  Pallas kernels  245 us (33%)
  waiting for transfers between devices  183 us (25%)
  matrix products  96.3 us (13%)
  local copies, waits for them, and re-layouts  84.6 us (11%)
  other arithmetic  60.6 us (8%)
  starting transfers between devices  41.5 us (6%)
  between operations  17.4 us (2%)
    pallas_call x3, Pallas kernels, comm_call(): pl.pallas_call(kernel, out_shape=outs, in_specs=[pl.BlockSpec(memory_spac...  245 us
    ppermute x24, waiting for transfers between devices, swap(): return lax.ppermute(x, axes, [(i, i ^ mask) for i in range(count)])  163 us
    dot_general x16, matrix products, dot(): return lax.dot_general(a, b, (dims, ((), ())), preferred_element_type=F32)  87 us
    ppermute x24, starting transfers between devices, swap(): return lax.ppermute(x, axes, [(i, i ^ mask) for i in range(count)])  33.4 us
    add x10, other arithmetic, reduce_axis(): total = total + swap(piece, (name,), m, sizes).astype(F32)  32.6 us
    unnamed x2, waiting for transfers between devices  19.8 us
    convert_element_type x6, local copies, waits for them, and re-layouts, from_members(): return g.reshape(rows, lead * nh * np_ * ny * nx * tail).astype(F32)  15.9 us
  transfers between devices with their start and end apart: 27, of which 12 were waited for; matrix products, arithmetic and copies ran while one was open for 20% of the time, Pallas kernels for 0%

profile of v2, /device:TPU:0, one launch (start us, length us, event | category | flops | bytes accessed | tf_op | source)
XLA Modules:
  0.0 728.3 jit_solution(4666479391163394628)
XLA Ops:
  12.6 6.1 concatenate.9
  25.5 90.3 %gather_first.1 = (bf16[4,128,2048]{2,1,0:T(8,128)(2,1)}, bf16[2,2,2,2,1,2,8,128]{7,6,5,4,3,2,1,0:T(8,128)(2,1)}, bf16[2,2,1,2,64,2048]{5,4,3,2,1,0:T(8,128)(2,1...) custom-call(bf16[128,2048]{1,0:T(8,128)(2,1)} %refs_0_.1, ...), custom_call_target="tpu_custom_call" | custom-call | tf_op jit(solution)/shard_map/gather_first/pallas_call | solution.py:116
  146.3 5.7 fusion.102
  152.0 61.6 %gather_second.1 = (bf16[3,128,2048]{2,1,0:T(8,128)(2,1)}, bf16[2,2,1,2,256,2048]{5,4,3,2,1,0:T(8,128)(2,1)}, bf16[2,2,64,2048]{3,2,1,0:T(8,128)(2,1)}) custom-call(bf16[4,128,2048]{2,1,0:T(8,128)(2,1)} %bitcast.234, bf16[256,2048]{1,0:T(8,128)(2,1)} %refs_1_.2, bf16[2,2,64,2048]{3,2,1,0:T(8,128)(2,1)} %reshape.633.refs_2_), custom_call_target="tpu_custom_call" | custom-call | tf_op jit(solution)/shard_map/gather_second/pallas_call | solution.py:116
  218.9 92.7 %gather_third.1 = (bf16[4,128,2048]{2,1,0:T(8,128)(2,1)}, bf16[4,128,2048]{2,1,0:T(8,128)(2,1)}, bf16[2,2,2,2,1,2,64,2048]{7,6,5,4,3,2,1,0:T(8,128)(2,1)}) custom-call(bf16[128,2048]{1,0:T(8,128)(2,1)} %add_convert_fusion.1.refs_0_, bf16[128,2048]{1,0:T(8,128)(2,1)} %refs_1_.3, bf16[2,2,64,2048]{3,2,1,0:T(8,128)(2,1)} %get-tuple-element.34.refs_2_), custom_call_target="tpu_custom_call" | custom-call | tf_op jit(solution)/shard_map/gather_third/pallas_call | solution.py:116
  311.7 7.7 %fusion.106 = f32[512,2048]{1,0:T(8,128)S(1)} fusion(bf16[512,2048]{1,0:T(8,128)(2,1)} %bitcast.301, bf16[2048,2048]{1,0:T(8,128)(2,1)} %bitcast.299), kind=kOutput, calls=%fused_computation.232 | convolution fusion | flops 4294967296 | bytes 14680064 | tf_op jit(solution)/shard_map/dot_general | solution.py:285
  319.4 12.3 %fusion.104 = (bf16[512,2048]{1,0:T(8,128)(2,1)S(1)}, f32[512,2048]{1,0:T(8,128)}) fusion(bf16[2048,2048]{1,0:T(8,128)(2,1)} %bitcast.295, f32[512,2048]{1,0:T(8,128)S(1)} %fusion.106, f32[2048]{0:T(1024)S(1)} %bitcast.284), kind=kOutput, calls=%fused_computation.230 | convolution fusion | flops 4306501632 | bytes 18882560 | tf_op jit(solution)/shard_map/dot_general | solution.py:285
  334.4 12.0 %collective-permute-start.2 = (bf16[128,2048]{1,0:T(8,128)(2,1)}, bf16[128,2048]{1,0:T(8,128)(2,1)}, u32[]{:S(2)}, u32[]{:S(2)}) collective-permute-start(bf16[128,2048]{1,0:T(8,128)(2,1)} %get-tuple-element.71), channel_id=1, source_target_pairs={{0,10},{2,8},{8,2},{10,0},{1,11},{3,9},{9,3},{11,1},{4,14},{6,12},... | collective-permute-start | bytes 1572872 | tf_op jit(solution)/shard_map/ppermute | solution.py:292
  346.4 8.8 %convert_reduce_fusion = (f32[2048]{0:T(1024)S(1)}, bf16[512,2048]{1,0:T(8,128)(2,1)S(1)}) fusion(f32[512,2048]{1,0:T(8,128)} %copy-done.40, f32[2048]{0:T(1024)S(1)} %bitcast.285, bf16[512,2048]{1,0:T(8,128)(2,1)S(1)} %bitcast.304, bf16[2048,2048]{1,0:T(8,128)(2,1)S(1)} %bitcast.298), kind=kOutput, calls=%fused_computation.28 | convolution fusion | flops 4319082496 | bytes 16793600 | tf_op jit(solution)/shard_map/dot_general | solution.py:285
  355.2 10.4 %fusion.103 = (bf16[512,2048]{1,0:T(8,128)(2,1)S(1)}, f32[512,2048]{1,0:T(8,128)}) fusion(bf16[512,2048]{1,0:T(8,128)(2,1)S(1)} %get-tuple-element.48, bf16[2048,2048]{1,0:T(8,128)(2,1)} %bitcast.300), kind=kOutput, calls=%fused_computation.229 | convolution fusion | flops 4296015872 | bytes 16777216 | tf_op jit(solution)/shard_map/dot_general | solution.py:285
  370.3 11.7 %convolution_convert_fusion = bf16[2048,2048]{1,0:T(8,128)(2,1)} fusion(bf16[512,2048]{1,0:T(8,128)(2,1)} %bitcast.303, f32[512,2048]{1,0:T(8,128)} %copy-done.40, f32[2048]{0:T(1024)S(1)} %bitcast.286), kind=kOutput, calls=%fused_computation.3 | convolution fusion | flops 4309647360 | bytes 14688256 | tf_op jit(solution)/shard_map/dot_general | solution.py:285
  382.0 7.0 convolution_convert_fusion.1
  389.1 6.7 constant_dynamic-slice_fusion.1
  406.0 9.9 %collective-permute-done.1 = bf16[128,2048]{1,0:T(8,128)(2,1)S(1)} collective-permute-done((bf16[128,2048]{1,0:T(8,128)(2,1)S(1)}, bf16[128,2048]{1,0:T(8,128)(2,1)S(1)}, u32[]{:S(2)}, u32[]{:S(2)}) %collective-permute-start.1) | collective-permute-done | bytes 524320 | tf_op jit(solution)/shard_map/ppermute | solution.py:292
  425.2 10.0 %collective-permute-done.8 = bf16[128,2048]{1,0:T(8,128)(2,1)S(1)} collective-permute-done((bf16[128,2048]{1,0:T(8,128)(2,1)S(1)}, bf16[128,2048]{1,0:T(8,128)(2,1)S(1)}, u32[]{:S(2)}, u32[]{:S(2)}) %collective-permute-start.8) | collective-permute-done | bytes 524320 | tf_op jit(solution)/shard_map/ppermute | solution.py:292
  435.3 7.7 %collective-permute-done.7 = bf16[128,2048]{1,0:T(8,128)(2,1)S(1)} collective-permute-done((bf16[128,2048]{1,0:T(8,128)(2,1)S(1)}, bf16[128,2048]{1,0:T(8,128)(2,1)S(1)}, u32[]{:S(2)}, u32[]{:S(2)}) %collective-permute-start.7) | collective-permute-done | bytes 524320 | tf_op jit(solution)/shard_map/ppermute | solution.py:292
  472.5 12.8 %collective-permute-done.9 = bf16[128,2048]{1,0:T(8,128)(2,1)} collective-permute-done((bf16[128,2048]{1,0:T(8,128)(2,1)}, bf16[128,2048]{1,0:T(8,128)(2,1)}, u32[]{:S(2)}, u32[]{:S(2)}) %collective-permute-start.9) | collective-permute-done | bytes 524320 | tf_op jit(solution)/shard_map/ppermute | solution.py:292
  490.4 10.8 %collective-permute-done.11 = bf16[128,2048]{1,0:T(8,128)(2,1)S(1)} collective-permute-done((bf16[128,2048]{1,0:T(8,128)(2,1)}, bf16[128,2048]{1,0:T(8,128)(2,1)S(1)}, u32[]{:S(2)}, u32[]{:S(2)}) %collective-permute-start.11) | collective-permute-done | bytes 524320 | tf_op jit(solution)/shard_map/ppermute | solution.py:292
  501.7 8.1 %collective-permute-done.10 = bf16[128,2048]{1,0:T(8,128)(2,1)S(1)} collective-permute-done((bf16[128,2048]{1,0:T(8,128)(2,1)S(1)}, bf16[128,2048]{1,0:T(8,128)(2,1)S(1)}, u32[]{:S(2)}, u32[]{:S(2)}) %collective-permute-start.10) | collective-permute-done | bytes 524320 | tf_op jit(solution)/shard_map/ppermute | solution.py:292
  539.3 19.6 %collective-permute-done.13 = bf16[2,2,2,64,1536]{4,3,2,1,0:T(8,128)(2,1)} collective-permute-done((bf16[2,2,2,64,1536]{4,3,2,1,0:T(8,128)(2,1)}, bf16[2,2,2,64,1536]{4,3,2,1,0:T(8,128)(2,1)}, u32[]{:S(2)}, u32[]{:S(2)}) %collective-permute-start.13) | collective-permute-done | bytes 1572896 | tf_op jit(solution)/shard_map/ppermute | solution.py:292
  563.2 40.7 %collective-permute-done.19 = bf16[2,2,2,64,2048]{4,3,2,1,0:T(8,128)(2,1)} collective-permute-done((bf16[2,2,2,64,2048]{4,3,2,1,0:T(8,128)(2,1)}, bf16[2,2,2,64,2048]{4,3,2,1,0:T(8,128)(2,1)}, u32[]{:S(2)}, u32[]{:S(2)}) %collective-permute-start.19) | collective-permute-done | bytes 2097184 | tf_op jit(solution)/shard_map/ppermute | solution.py:292
  615.5 30.8 %collective-permute-done.22 = bf16[2,256,2048]{2,1,0:T(8,128)(2,1)} collective-permute-done((bf16[2,256,2048]{2,1,0:T(8,128)(2,1)}, bf16[2,256,2048]{2,1,0:T(8,128)(2,1)}, u32[]{:S(2)}, u32[]{:S(2)}) %collective-permute-start.22) | collective-permute-done | bytes 2097184 | tf_op jit(solution)/shard_map/ppermute | solution.py:292
  664.5 19.8 %all-reduce.4.cloned.1.call-done = f32[32,768]{1,0:T(8,128)} async-done(((f32[32,768]{1,0:T(8,128)}), f32[32,768]{1,0:T(8,128)}) %all-reduce.4.cloned.1.call-update) | async-done | bytes 98320
  689.1 12.3 %collective-permute-done.23 = bf16[256,2048]{1,0:T(8,128)(2,1)} collective-permute-done((bf16[256,2048]{1,0:T(8,128)(2,1)}, bf16[256,2048]{1,0:T(8,128)(2,1)}, u32[]{:S(2)}, u32[]{:S(2)}) %collective-permute-start.23) | collective-permute-done | bytes 1048608 | tf_op jit(solution)/shard_map/ppermute | solution.py:292
  (284 shorter events, 195.4 us)
Async XLA Ops:
  7.2 677.2 %all-reduce.4.cloned.1.call-start = ((), (), s32[]{:S(2)}) async-start(), calls=%async_computation.2 | async-start | bytes 196608
  333.0 73.0 %collective-permute-start = (bf16[128,2048]{1,0:T(8,128)(2,1)}, bf16[128,2048]{1,0:T(8,128)(2,1)}, u32[]{:S(2)}, u32[]{:S(2)}) collective-permute-start(bf16[128,2048]{1,0:T(8,128)(2,1)} %get-tuple-element.70), channel_id=1, source_target_pairs={{0,2},{2,0},{8,10},{10,8},{1,3},{3,1},{9,11},{11,9},{4,6},{6,4},{1... | collective-permute-start | bytes 1572872 | tf_op jit(solution)/shard_map/ppermute | solution.py:292
  334.4 71.6 %collective-permute-start.2 = (bf16[128,2048]{1,0:T(8,128)(2,1)}, bf16[128,2048]{1,0:T(8,128)(2,1)}, u32[]{:S(2)}, u32[]{:S(2)}) collective-permute-start(bf16[128,2048]{1,0:T(8,128)(2,1)} %get-tuple-element.71), channel_id=1, source_target_pairs={{0,10},{2,8},{8,2},{10,0},{1,11},{3,9},{9,3},{11,1},{4,14},{6,12},... | collective-permute-start | bytes 1572872 | tf_op jit(solution)/shard_map/ppermute | solution.py:292
  366.8 36.1 %collective-permute-start.3 = (bf16[128,2048]{1,0:T(8,128)(2,1)}, bf16[128,2048]{1,0:T(8,128)(2,1)}, u32[]{:S(2)}, u32[]{:S(2)}) collective-permute-start(bf16[128,2048]{1,0:T(8,128)(2,1)} %get-tuple-element.67), channel_id=1, source_target_pairs={{0,2},{2,0},{8,10},{10,8},{1,3},{3,1},{9,11},{11,9},{4,6},{6,4},{1... | collective-permute-start | bytes 1572872 | tf_op jit(solution)/shard_map/ppermute | solution.py:292
  367.4 35.7 %collective-permute-start.5 = (bf16[128,2048]{1,0:T(8,128)(2,1)}, bf16[128,2048]{1,0:T(8,128)(2,1)}, u32[]{:S(2)}, u32[]{:S(2)}) collective-permute-start(bf16[128,2048]{1,0:T(8,128)(2,1)} %get-tuple-element.68), channel_id=1, source_target_pairs={{0,10},{2,8},{8,2},{10,0},{1,11},{3,9},{9,3},{11,1},{4,14},{6,12},... | collective-permute-start | bytes 1572872 | tf_op jit(solution)/shard_map/ppermute | solution.py:292
  367.4 35.7 %collective-permute-start.4 = (bf16[128,2048]{1,0:T(8,128)(2,1)}, bf16[128,2048]{1,0:T(8,128)(2,1)}, u32[]{:S(2)}, u32[]{:S(2)}) collective-permute-start(bf16[128,2048]{1,0:T(8,128)(2,1)} %get-tuple-element.69), channel_id=1, source_target_pairs={{0,8},{2,10},{8,0},{10,2},{1,9},{3,11},{9,1},{11,3},{4,12},{6,14},... | collective-permute-start | bytes 1572872 | tf_op jit(solution)/shard_map/ppermute | solution.py:292
  403.0 128.9 %collective-permute-start.21 = (bf16[2,2,1,256,2048]{4,3,0,2,1:T(8,128)(2,1)}, bf16[2,2,1,256,2048]{4,3,0,2,1:T(8,128)(2,1)}, u32[]{:S(2)}, u32[]{:S(2)}) collective-permute-start(bf16[2,2,1,256,2048]{4,3,0,2,1:T(8,128)(2,1)} %bitcast.221), channel_id=1, source_target_pairs={{0,1},{1,0},{2,3},{3,2},{4,5},{5,4},{6,7},{7,6},{8,9},{9,8},{10,11... | collective-permute-start | bytes 12582920 | tf_op jit(solution)/shard_map/ppermute | solution.py:292
  403.1 119.5 %collective-permute-start.18 = (bf16[2,2,2,2,1,64,2048]{6,5,3,2,1,0,4:T(8,128)(2,1)}, bf16[2,2,2,2,1,64,2048]{6,5,3,2,1,0,4:T(8,128)(2,1)}, u32[]{:S(2)}, u32[]{:S(2)}) collective-permute-start(bf16[2,2,2,2,1,64,2048]{6,5,3,2,1,0,4:T(8,128)(2,1)} %dynamic-slice_bitcast_fusion), channel_id=1, source_target_pairs={{0,1},{1,0},{2,3},{3,2},{4,5},{5,4},{6,7},{7,6},{8,9},{9,8},{10,11... | collective-permute-start | bytes 12582920 | tf_op jit(solution)/shard_map/ppermute | solution.py:292
  419.6 15.7 %collective-permute-start.8 = (bf16[128,2048]{1,0:T(8,128)(2,1)S(1)}, bf16[128,2048]{1,0:T(8,128)(2,1)S(1)}, u32[]{:S(2)}, u32[]{:S(2)}) collective-permute-start(bf16[128,2048]{1,0:T(8,128)(2,1)S(1)} %get-tuple-element.50), channel_id=1, source_target_pairs={{0,10},{2,8},{8,2},{10,0},{1,11},{3,9},{9,3},{11,1},{4,14},{6,12},... | collective-permute-start | bytes 1572872 | tf_op jit(solution)/shard_map/ppermute | solution.py:292
  419.9 23.1 %collective-permute-start.7 = (bf16[128,2048]{1,0:T(8,128)(2,1)S(1)}, bf16[128,2048]{1,0:T(8,128)(2,1)S(1)}, u32[]{:S(2)}, u32[]{:S(2)}) collective-permute-start(bf16[128,2048]{1,0:T(8,128)(2,1)S(1)} %get-tuple-element.50), channel_id=1, source_target_pairs={{0,8},{2,10},{8,0},{10,2},{1,9},{3,11},{9,1},{11,3},{4,12},{6,14},... | collective-permute-start | bytes 1572872 | tf_op jit(solution)/shard_map/ppermute | solution.py:292
  421.6 22.1 %collective-permute-start.6 = (bf16[128,2048]{1,0:T(8,128)(2,1)S(1)}, bf16[128,2048]{1,0:T(8,128)(2,1)S(1)}, u32[]{:S(2)}, u32[]{:S(2)}) collective-permute-start(bf16[128,2048]{1,0:T(8,128)(2,1)S(1)} %get-tuple-element.50), channel_id=1, source_target_pairs={{0,2},{2,0},{8,10},{10,8},{1,3},{3,1},{9,11},{11,9},{4,6},{6,4},{1... | collective-permute-start | bytes 1572872 | tf_op jit(solution)/shard_map/ppermute | solution.py:292
  459.0 26.9 %collective-permute-start.15 = (bf16[2,2,1,64,2048]{4,3,0,2,1:T(8,128)(2,1)S(1)}, bf16[2,2,1,64,2048]{4,3,0,2,1:T(8,128)(2,1)}, u32[]{:S(2)}, u32[]{:S(2)}) collective-permute-start(bf16[2,2,1,64,2048]{4,3,0,2,1:T(8,128)(2,1)S(1)} %bitcast.270), channel_id=1, source_target_pairs={{0,1},{1,0},{2,3},{3,2},{4,5},{5,4},{6,7},{7,6},{8,9},{9,8},{10,11... | collective-permute-start | bytes 3145736 | tf_op jit(solution)/shard_map/ppermute | solution.py:292
  465.5 49.8 %collective-permute-start.12 = (bf16[2,2,2,2,1,64,1536]{6,5,3,2,1,0,4:T(8,128)(2,1)}, bf16[2,2,2,2,1,64,1536]{6,5,3,2,1,0,4:T(8,128)(2,1)}, u32[]{:S(2)}, u32[]{:S(2)}) collective-permute-start(bf16[2,2,2,2,1,64,1536]{6,5,3,2,1,0,4:T(8,128)(2,1)} %dynamic-slice_bitcast_fusion.1), channel_id=1, source_target_pairs={{0,1},{1,0},{2,3},{3,2},{4,5},{5,4},{6,7},{7,6},{8,9},{9,8},{10,11... | collective-permute-start | bytes 9437192 | tf_op jit(solution)/shard_map/ppermute | solution.py:292
  485.3 15.9 %collective-permute-start.11 = (bf16[128,2048]{1,0:T(8,128)(2,1)}, bf16[128,2048]{1,0:T(8,128)(2,1)S(1)}, u32[]{:S(2)}, u32[]{:S(2)}) collective-permute-start(bf16[128,2048]{1,0:T(8,128)(2,1)} %get-tuple-element.65), channel_id=1, source_target_pairs={{0,10},{2,8},{8,2},{10,0},{1,11},{3,9},{9,3},{11,1},{4,14},{6,12},... | collective-permute-start | bytes 1572872 | tf_op jit(solution)/shard_map/ppermute | solution.py:292
  486.0 23.9 %collective-permute-start.10 = (bf16[128,2048]{1,0:T(8,128)(2,1)S(1)}, bf16[128,2048]{1,0:T(8,128)(2,1)S(1)}, u32[]{:S(2)}, u32[]{:S(2)}) collective-permute-start(bf16[128,2048]{1,0:T(8,128)(2,1)S(1)} %get-tuple-element.66), channel_id=1, source_target_pairs={{0,8},{2,10},{8,0},{10,2},{1,9},{3,11},{9,1},{11,3},{4,12},{6,14},... | collective-permute-start | bytes 1572872 | tf_op jit(solution)/shard_map/ppermute | solution.py:292
  521.0 37.8 %collective-permute-start.13 = (bf16[2,2,2,64,1536]{4,3,2,1,0:T(8,128)(2,1)}, bf16[2,2,2,64,1536]{4,3,2,1,0:T(8,128)(2,1)}, u32[]{:S(2)}, u32[]{:S(2)}) collective-permute-start(bf16[2,2,2,64,1536]{4,3,2,1,0:T(8,128)(2,1)} %fusion.17), channel_id=1, source_target_pairs={{0,4},{4,0},{1,5},{5,1},{2,6},{6,2},{3,7},{7,3},{8,12},{12,8},{9,1... | collective-permute-start | bytes 4718600 | tf_op jit(solution)/shard_map/ppermute | solution.py:292
  528.2 75.7 %collective-permute-start.19 = (bf16[2,2,2,64,2048]{4,3,2,1,0:T(8,128)(2,1)}, bf16[2,2,2,64,2048]{4,3,2,1,0:T(8,128)(2,1)}, u32[]{:S(2)}, u32[]{:S(2)}) collective-permute-start(bf16[2,2,2,64,2048]{4,3,2,1,0:T(8,128)(2,1)} %fusion.12), channel_id=1, source_target_pairs={{0,4},{4,0},{1,5},{5,1},{2,6},{6,2},{3,7},{7,3},{8,12},{12,8},{9,1... | collective-permute-start | bytes 6291464 | tf_op jit(solution)/shard_map/ppermute | solution.py:292
  531.4 155.8 %collective-permute-start.17 = (bf16[64,2048]{1,0:T(8,128)(2,1)}, bf16[64,2048]{1,0:T(8,128)(2,1)}, u32[]{:S(2)}, u32[]{:S(2)}) collective-permute-start(bf16[64,2048]{1,0:T(8,128)(2,1)} %fusion.79), channel_id=1, source_target_pairs={{0,16},{16,0},{1,17},{17,1},{2,18},{18,2},{3,19},{19,3},{4,20},{20... | collective-permute-start | bytes 786440 | tf_op jit(solution)/shard_map/ppermute | solution.py:292
  537.8 108.4 %collective-permute-start.22 = (bf16[2,256,2048]{2,1,0:T(8,128)(2,1)}, bf16[2,256,2048]{2,1,0:T(8,128)(2,1)}, u32[]{:S(2)}, u32[]{:S(2)}) collective-permute-start(bf16[2,256,2048]{2,1,0:T(8,128)(2,1)} %fusion.13), channel_id=1, source_target_pairs={{0,4},{4,0},{1,5},{5,1},{2,6},{6,2},{3,7},{7,3},{8,12},{12,8},{9,1... | collective-permute-start | bytes 6291464 | tf_op jit(solution)/shard_map/ppermute | solution.py:292
  561.8 49.1 %collective-permute-start.14 = (bf16[2,2,64,1536]{3,2,1,0:T(8,128)(2,1)S(1)}, bf16[2,2,64,1536]{3,2,1,0:T(8,128)(2,1)S(1)}, u32[]{:S(2)}, u32[]{:S(2)}) collective-permute-start(bf16[2,2,64,1536]{3,2,1,0:T(8,128)(2,1)S(1)} %fusion.67), channel_id=1, source_target_pairs={{0,16},{16,0},{1,17},{17,1},{2,18},{18,2},{3,19},{19,3},{4,20},{20... | collective-permute-start | bytes 2359304 | tf_op jit(solution)/shard_map/ppermute | solution.py:292
  609.5 46.7 %collective-permute-start.20 = (bf16[2,2,64,2048]{3,2,1,0:T(8,128)(2,1)}, bf16[2,2,64,2048]{3,2,1,0:T(8,128)(2,1)}, u32[]{:S(2)}, u32[]{:S(2)}) collective-permute-start(bf16[2,2,64,2048]{3,2,1,0:T(8,128)(2,1)} %fusion.56), channel_id=1, source_target_pairs={{0,16},{16,0},{1,17},{17,1},{2,18},{18,2},{3,19},{19,3},{4,20},{20... | collective-permute-start | bytes 3145736 | tf_op jit(solution)/shard_map/ppermute | solution.py:292
  612.0 46.7 %all-to-all-start = ((bf16[4,64,1536]{2,1,0:T(8,128)(2,1)}), bf16[4,64,1536]{2,1,0:T(8,128)(2,1)S(1)}, u32[]{:S(2)}, u32[]{:S(2)}) async-start(bf16[4,64,1536]{2,1,0:T(8,128)(2,1)} %bitcast.254), calls=%async_computation | async-start | bytes 1572864 | tf_op jit(solution)/shard_map/all_to_all | solution.py:497
  654.8 46.6 %collective-permute-start.23 = (bf16[256,2048]{1,0:T(8,128)(2,1)}, bf16[256,2048]{1,0:T(8,128)(2,1)}, u32[]{:S(2)}, u32[]{:S(2)}) collective-permute-start(bf16[256,2048]{1,0:T(8,128)(2,1)} %fusion.57), channel_id=1, source_target_pairs={{0,16},{16,0},{1,17},{17,1},{2,18},{18,2},{3,19},{19,3},{4,20},{20... | collective-permute-start | bytes 3145736 | tf_op jit(solution)/shard_map/ppermute | solution.py:292
  658.7 52.2 %all-to-all-start.1 = ((bf16[4,64,2048]{2,1,0:T(8,128)(2,1)}), bf16[4,64,2048]{2,1,0:T(8,128)(2,1)}, u32[]{:S(2)}, u32[]{:S(2)}) async-start(bf16[4,64,2048]{2,1,0:T(8,128)(2,1)} %bitcast.72), calls=%async_computation.1 | async-start | bytes 2097152 | tf_op jit(solution)/shard_map/all_to_all | solution.py:497
  (50 other events, 796.9 us)
Sparse Core Ops, SparseCore 0:
  512.9 171.3 all-reduce.3
